TPU v7x, 128 devices: a whole 4x4x4 slice. The times are simulated.
128 devices in a mesh: gx: 8 (over y, core), gy: 16 (over z, x).
Axes of the slice: x: 4, y: 4, z: 4, core: 2. Of those that a mesh axis runs over, the one named last changes fastest.
Arguments:
- density: float32 [32, 2048, 4096], P(None, 'gx', 'gy'), may hold values from -6 to 6
- spacing_x: float32 [2048], replicated, may hold values from 0.5 to 2
- spacing_y: float32 [4096], replicated, may hold values from 0.5 to 2
Outputs:
- detail: float32 [32, 2048, 4096], P(None, 'gx', 'gy')
- coarse_new: float32 [32, 1024, 2048], P(None, 'gx', 'gy')
All inputs are finite; a program needn't handle non-finite values.
Results may differ from a plain program's by a relative error of at most 0.0003.
Values sent between devices are 32-bit elements; how exact they have to be, the bound alone decides.
A program may use at most 192 MiB of HBM per device.

v0:
```python
import functools

import jax
import jax.numpy as jnp
from jax import lax
from jax.experimental import pallas as pl
from jax.experimental.pallas import tpu as pltpu
from jax.sharding import PartitionSpec as P

MESH = pl.DeviceIdType.MESH
F32 = jnp.float32
BF16 = jnp.bfloat16
HIGHEST = lax.Precision.HIGHEST
stiffness_weight = 4096.0
operator_divisor = 32.0
LANES = 128
FINE = 256
PLANES = 32
STEP = 4
MIB = 1 << 20
X_WL, X_WR, X_K1, X_K2, X_K3, X_K4, X_K5, X_U, X_PSI, X_W = range(10)
Y_K1, Y_K2, Y_K3, Y_K4, Y_K5, Y_U, Y_W = range(10, 17)
S_FX, S_BX, S_FY, S_BY, S_WRM, S_UY, S_PSIY = range(7)


def split(values):
    high = values.astype(BF16)
    return high, (values - high.astype(F32)).astype(BF16)


def mxu(a, b):
    return jnp.dot(a, b, preferred_element_type=F32)


def iota(shape, dim):
    return lax.broadcasted_iota(jnp.int32, shape, dim)


def column(table, index):
    return jnp.broadcast_to(table[:, index : index + 1], (LANES, LANES))


def shift_up(values, last):
    rolled = pltpu.roll(values, LANES - 1, 0)
    return jnp.where(iota(values.shape, 0) == LANES - 1, last, rolled)


def shift_down(values, first):
    return jnp.where(iota(values.shape, 0) == 0, first, pltpu.roll(values, 1, 0))


def chain_tables(blocks_x, blocks_y, sx, sy, tab, rows_in):
    count = blocks_x + blocks_y
    shape = (count, LANES)
    lane, row = iota(shape, 1), iota(shape, 0)
    first = (lane == 0) & ((row == 0) | (row == blocks_x))

    def prev(values, fill):
        rolled = pltpu.roll(values, 1, 1)
        return jnp.where(first, fill, jnp.where(lane == 0, pltpu.roll(rolled, 1, 0), rolled))

    def following(values):
        rolled = pltpu.roll(values, LANES - 1, 1)
        return jnp.where(lane == LANES - 1, pltpu.roll(rolled, count - 1, 0), rolled)

    def halves(start):
        return jnp.concatenate(
            [sx[pl.ds(start, blocks_x, stride=2), :], sy[pl.ds(start, blocks_y, stride=2), :]], axis=0
        )

    fine = jnp.concatenate([halves(0), halves(1)], axis=1)
    node, place = iota((FINE, FINE), 0), iota((FINE, FINE), 1)
    pick = jnp.where(place < LANES, 2 * place, 2 * (place - LANES) + 1)
    parts = jnp.dot((fine), (node == pick).astype(F32), precision=HIGHEST, preferred_element_type=F32)
    c, d = parts[:, :LANES], parts[:, LANES:]
    span = c + d
    a, b = prev(c, 0.0), prev(d, 0.0)
    span_before = prev(span, 1.0)
    inverse = 1.0 / span
    inverse_before = 1.0 / span_before
    tab[0] = d * inverse
    tab[1] = c * inverse
    tab[2] = a * a * inverse_before * (1.0 / 6.0)
    tab[3] = a * (1.0 / 3.0) + b * (1.0 / 6.0)
    tab[4] = (a * b * inverse_before + c * d * inverse) * (1.0 / 6.0) + (b + c) * (1.0 / 3.0)
    tab[5] = c * (1.0 / 6.0) + d * (1.0 / 3.0)
    tab[6] = d * d * inverse * (1.0 / 6.0)
    tab[9] = b * inverse_before
    tab[10] = a * inverse_before

    rho = 1.0 / (stiffness_weight * inverse - span * (1.0 / 6.0))
    rho_before = prev(rho, 0.0)
    mu = 0.5 * (a + b + span)
    mu_after = following(mu)
    one = jnp.ones(shape, F32)
    fwd = (one + mu * rho_before, mu, rho_before, one)
    bwd = (one, mu_after, rho, one + rho * mu_after)
    step = 1
    while step < LANES:
        def join(m, shift, outside):
            fill = (1.0, 0.0, 0.0, 1.0)
            a1, b1, c1, d1 = m
            a0, b0, c0, d0 = (
                jnp.where(outside, f, pltpu.roll(v, shift, 1)) for v, f in zip(m, fill)
            )
            return (a1 * a0 + b1 * c0, a1 * b0 + b1 * d0, c1 * a0 + d1 * c0, c1 * b0 + d1 * d0)

        fwd = join(fwd, step, lane < step)
        bwd = join(bwd, LANES - step, lane >= LANES - step)
        step *= 2
    ends = [jnp.broadcast_to(v[:, LANES - 1 : LANES], shape) for v in fwd]
    starts = [jnp.broadcast_to(v[:, 0:1], shape) for v in bwd]
    for low, size in ((0, blocks_x), (blocks_x, blocks_y)):
        y = jnp.zeros((1, LANES), F32)
        for q in range(low, low + size):
            rows_in[0, q : q + 1, :] = y
            at, bt, ct, dt = (v[q : q + 1, :] for v in ends)
            y = (at * y + bt) / (ct * y + dt)
        z = None
        for q in reversed(range(low, low + size)):
            at, bt, ct, dt = (v[q : q + 1, :] for v in starts)
            if z is None:
                rows_in[1, q : q + 1, :] = jnp.ones((1, LANES), F32)
                rows_in[2, q : q + 1, :] = jnp.zeros((1, LANES), F32)
                z = at / ct
            else:
                rows_in[1, q : q + 1, :] = z
                rows_in[2, q : q + 1, :] = jnp.ones((1, LANES), F32)
                z = (at * z + bt) / (ct * z + dt)
    y_in, z_num, z_den = rows_in[0], rows_in[1], rows_in[2]
    den = fwd[2] * y_in + fwd[3]
    left = (fwd[0] * y_in + fwd[1]) / den
    right = (bwd[0] * z_num + bwd[1] * z_den) / (bwd[2] * z_num + bwd[3] * z_den)
    green = operator_divisor / (left + right)
    tab[7] = green / den
    tab[8] = den
    tab[11] = 1.0 / jnp.broadcast_to(den[:, LANES - 1 : LANES], shape)
    tab[12] = 1.0 / jnp.broadcast_to(green[:, LANES - 1 : LANES], shape)
    tab[13] = 1.0 / jnp.broadcast_to(den[:, 0:1], shape)


def weights_between(gain, low, size, own, forward, backward):
    q = iota((size, LANES), 0)
    ahead = jnp.ones((size, LANES), F32)
    behind = jnp.ones((size, LANES), F32)
    for m in range(size):
        g = gain[low + m : low + m + 1, :]
        ahead = ahead * jnp.where((m > q) & (m < own), g, 1.0)
        behind = behind * jnp.where((m < q) & (m > own), g, 1.0)
    forward[low : low + size, :] = jnp.where(q < own, ahead, 0.0)
    backward[low : low + size, :] = jnp.where(q > own, behind, 0.0)


def green_block(u_col, w_col, u_row, w_row):
    i, j = iota((LANES, LANES), 0), iota((LANES, LANES), 1)
    return jnp.where(i >= j, u_col * w_row, w_col * u_row)


def prepare_kernel(
    nx, ny, dens, sx, sy,
    colx, ycoef, scal, cf, cb, wcat, gxh, gxl, rh, er, lch, lcl,
    box, rsend, csend, rrecv, cl, cr, tiles, tab, rows_in, stack, wfine, merged, load_sem, send_sem, recv_sem,
):
    p, r = lax.axis_index("gx"), lax.axis_index("gy")
    up, down = lax.rem(p + nx - 1, nx), lax.rem(p + 1, nx)
    left, right = lax.rem(r + ny - 1, ny), lax.rem(r + 1, ny)
    loads = []
    for k in range(PLANES // STEP):
        part = pl.ds(k * STEP, STEP)
        loads.append(pltpu.make_async_copy(dens.at[part], box.at[part], load_sem.at[k]))
        loads[-1].start()
    barrier = pltpu.get_barrier_semaphore()
    for i in (up, p, down):
        for j in (left, r, right):
            if i is p and j is r:
                continue
            pl.semaphore_signal(barrier, inc=1, device_id=(i, j), device_id_type=MESH)

    lane_f = iota((FINE, LANES), 1)
    csend[...] = jnp.zeros((FINE, LANES), F32)
    for k in range(PLANES // STEP):
        loads[k].wait()
        acc = csend[...]
        for zi in range(STEP):
            z = k * STEP + zi
            acc = jnp.where(lane_f == z, box[z, :, FINE - 2 : FINE - 1], acc)
            acc = jnp.where(lane_f == PLANES + z, box[z, :, FINE - 1 : FINE], acc)
            acc = jnp.where(lane_f == 2 * PLANES + z, box[z, :, 0:1], acc)
            rsend[0, z : z + 1, :] = box[z, FINE - 2 : FINE - 1, :]
            rsend[1, z : z + 1, :] = box[z, FINE - 1 : FINE, :]
            rsend[2, z : z + 1, :] = box[z, 0:1, :]
        csend[...] = acc

    pl.semaphore_wait(barrier, 8)
    top, bottom = pl.ds(0, 8), pl.ds(FINE - 8, 8)
    plan = (
        (rsend.at[pl.ds(0, 2)], rrecv.at[pl.ds(0, 2)], down, r),
        (rsend.at[pl.ds(2, 1)], rrecv.at[pl.ds(2, 1)], up, r),
        (csend, cl, p, right),
        (csend, cr, p, left),
        (csend.at[bottom], tiles.at[0], down, r),
        (csend.at[top], tiles.at[1], up, r),
        (csend.at[bottom], tiles.at[2], down, right),
        (csend.at[bottom], tiles.at[3], down, left),
        (csend.at[top], tiles.at[4], up, right),
        (csend.at[top], tiles.at[5], up, left),
    )
    copies = []
    for k, (src, dst, i, j) in enumerate(plan):
        copies.append(
            pltpu.make_async_remote_copy(
                src_ref=src, dst_ref=dst, send_sem=send_sem.at[k], recv_sem=recv_sem.at[k],
                device_id=(i, j), device_id_type=MESH,
            )
        )
        copies[-1].start()

    chain_tables(nx, ny, sx, sy, tab, rows_in)
    weights_between(tab[11], 0, nx, p, cf, cb)
    weights_between(tab[11], nx, ny, r, cf, cb)
    row_x, row_y = pl.ds(p, 1), pl.ds(nx + r, 1)
    ux, wx, uy, wy = tab[7, row_x, :], tab[8, row_x, :], tab[7, row_y, :], tab[8, row_y, :]
    stack[...] = jnp.zeros((LANES, LANES), F32)
    for k in range(7):
        stack[k : k + 1, :] = tab[k, row_x, :]
    stack[X_U : X_U + 1, :] = ux
    stack[X_PSI : X_PSI + 1, :] = wx * tab[11, row_x, :]
    stack[X_W : X_W + 1, :] = wx
    for k in range(5):
        stack[Y_K1 + k : Y_K1 + k + 1, :] = tab[2 + k, row_y, :]
    stack[Y_U : Y_U + 1, :] = uy
    stack[Y_W : Y_W + 1, :] = wy
    cols = stack[...].T
    colx[...] = cols
    scal[...] = jnp.zeros((8, LANES), F32)
    scal[S_FX : S_FX + 1, :] = tab[12, row_x, :]
    scal[S_BX : S_BX + 1, :] = tab[13, row_x, :]
    scal[S_FY : S_FY + 1, :] = tab[12, row_y, :]
    scal[S_BY : S_BY + 1, :] = tab[13, row_y, :]
    wl_x = tab[9, row_x, :][:, 0:1]
    wr_x = tab[10, row_x, :][:, 0:1]
    wl_y = tab[9, row_y, :][:, 0:1]
    wr_y = tab[10, row_y, :][:, 0:1]
    scal[S_WRM : S_WRM + 1, :] = jnp.broadcast_to(wr_x, (1, LANES))
    scal[S_UY : S_UY + 1, :] = uy
    scal[S_PSIY : S_PSIY + 1, :] = wy * tab[11, row_y, :]

    odd_row = (iota((1, LANES), 1) & 1) == 1
    ycoef[...] = jnp.zeros((8, FINE), F32)
    for t in range(2):
        h = sy[pl.ds(2 * r + t, 1), :]
        hp = pltpu.roll(h, 1, 1)
        inv = 1.0 / (h + hp)
        ycoef[0:1, t * LANES : (t + 1) * LANES] = jnp.where(odd_row, h * inv, 0.0)
        ycoef[1:2, t * LANES : (t + 1) * LANES] = jnp.where(odd_row, hp * inv, 0.0)

    hi, lo = split(green_block(column(cols, X_U), column(cols, X_W), ux, wx))
    gxh[...] = hi
    gxl[...] = lo
    gy = green_block(column(cols, Y_U), column(cols, Y_W), uy, wy)
    g1, g2, g3, g4, g5 = (column(cols, Y_K1 + k) * gy for k in range(5))
    wfine[pl.ds(0, LANES, stride=2), :] = g3 + shift_down(g5, 0.0) + shift_up(g1, 0.0)
    wfine[pl.ds(1, LANES, stride=2), :] = g4 + shift_up(g2, 0.0)
    i = iota((LANES, LANES), 0)
    outer = jnp.where(
        i < PLANES, g1[0:1, :],
        jnp.where(i < 2 * PLANES, g2[0:1, :], jnp.where(i < 3 * PLANES, g5[LANES - 1 : LANES, :], 0.0)),
    )
    hi, lo = split(wfine[...])
    wcat[0:FINE, 0:LANES] = hi
    wcat[0:FINE, LANES:FINE] = lo
    hi, lo = split(outer)
    wcat[FINE : FINE + LANES, 0:LANES] = hi
    wcat[FINE : FINE + LANES, LANES:FINE] = lo

    for copy in copies:
        copy.wait()

    has_up = (p > 0).astype(F32)
    has_down = (p < nx - 1).astype(F32)
    has_left = (r > 0).astype(F32)
    has_right = (r < ny - 1).astype(F32)
    lane_8 = iota((8, LANES), 1)
    lane = iota((LANES, LANES), 1)
    merged[...] = jnp.where(lane_f < 2 * PLANES, cl[...] * has_left, cr[...] * has_right)
    e_c, o_c = merged[pl.ds(0, LANES, stride=2), :], merged[pl.ds(1, LANES, stride=2), :]
    own = csend[pl.ds(0, LANES, stride=2), :]
    own_n, own_s = tiles[0] * has_up, tiles[1] * has_down
    north = jnp.where(lane_8 < 2 * PLANES, tiles[2] * has_left, tiles[3] * has_right) * has_up
    south = jnp.where(lane_8 < 2 * PLANES, tiles[4] * has_left, tiles[5] * has_right) * has_down

    def along_y(values, own_values):
        at = iota(values.shape, 1)
        guess = wl_y * pltpu.roll(values, PLANES, 1) + wr_y * pltpu.roll(own_values, LANES - PLANES, 1)
        return jnp.where((at >= PLANES) & (at < 2 * PLANES), guess, values)

    se = along_y(e_c, own)
    se_n = along_y(north, own_n)[6:7, :]
    se_s = along_y(south, own_s)[0:1, :]
    do = o_c - (column(cols, X_WL) * se + column(cols, X_WR) * shift_up(se, se_s))
    de = e_c - se
    de_n = north[6:7, :] - se_n
    do_n = north[7:8, :] - (wl_x * se_n + wr_x * se[0:1, :])
    de_s = south[0:1, :] - se_s
    loads_c = (
        column(cols, X_K1) * shift_down(de, de_n)
        + column(cols, X_K2) * shift_down(do, do_n)
        + column(cols, X_K3) * de
        + column(cols, X_K4) * do
        + column(cols, X_K5) * shift_up(de, de_s)
    )
    hi, lo = split(loads_c)
    lch[...] = hi
    lcl[...] = lo
    er[...] = e_c

    stack[0:8, :] = north
    stack[8:16, :] = south
    corner = stack[...].T
    corner_n = corner[2 * PLANES : 3 * PLANES, 6:7]
    corner_s = corner[2 * PLANES : 3 * PLANES, 8:9]
    lane_z = iota((PLANES, LANES), 1)
    odd = (lane_z & 1) == 1

    def row_along_y(layer, scale, corner_col):
        tiles_in = [layer[:, t * LANES : (t + 1) * LANES] * scale for t in range(2)]
        next_in = [pltpu.roll(v, LANES - 1, 1) for v in tiles_in]
        after = [
            jnp.where(lane_z < LANES - 1, next_in[0], next_in[1]),
            jnp.where(lane_z < LANES - 1, next_in[1], corner_col),
        ]
        result = []
        for t in range(2):
            part = slice(t * LANES, (t + 1) * LANES)
            guess = ycoef[0:1, part] * pltpu.roll(tiles_in[t], 1, 1) + ycoef[1:2, part] * after[t]
            result.append(jnp.where(odd, guess, tiles_in[t]))
        return tiles_in, result

    e_n, s_n = row_along_y(rrecv[0], has_up, corner_n)
    e_s, s_s = row_along_y(rrecv[2], has_down, corner_s)
    for t in range(2):
        part = slice(t * LANES, (t + 1) * LANES)
        rh[0, t] = e_n[t] - s_n[t]
        rh[1, t] = rrecv[1, :, part] * has_up - wl_x * s_n[t]
        rh[2, t] = s_s[t]
        rh[3, t] = e_s[t] - s_s[t]


def main_kernel(
    dens_l, dens_r, colx, ycoef, scal, rh, er, lch, lcl, wcat, gxh, gxl,
    detail, local, coarse, wide, se_buf, de_buf, do_buf, woven,
):
    g = pl.program_id(0)

    @pl.when(g == 0)
    def _():
        for k in range(7):
            wide[k] = column(colx[...], k)

    lane = iota((LANES, LANES), 1)
    odd = (lane & 1) == 1
    inner = lane < LANES - 1
    pick = (2 * lane) & (LANES - 1)
    wrm = scal[S_WRM : S_WRM + 1, :]
    body, before, after = pl.ds(8, LANES), pl.ds(7, LANES), pl.ds(9, LANES)

    def plane(zi, z):
        row = pl.ds(z, 1)
        parts = [slice(t * LANES, (t + 1) * LANES) for t in range(2)]
        e = [dens[zi, pl.ds(0, LANES, stride=2), :] for dens in (dens_l, dens_r)]
        o = [dens[zi, pl.ds(1, LANES, stride=2), :] for dens in (dens_l, dens_r)]
        nxt = [pltpu.roll(v, LANES - 1, 1) for v in e]
        beyond = pltpu.roll(er[...], lax.rem(3 * LANES - 1 - 2 * PLANES - z, LANES), 1)
        nxt = [jnp.where(inner, nxt[0], nxt[1]), jnp.where(inner, nxt[1], beyond)]
        high, low = [], []
        for t in range(2):
            part = parts[t]
            guess = ycoef[0:1, part] * pltpu.roll(e[t], 1, 1) + ycoef[1:2, part] * nxt[t]
            se = jnp.where(odd, guess, e[t])
            de = e[t] - se
            se_buf[t, body, :] = se
            se_buf[t, pl.ds(8 + LANES, 1), :] = rh[2, t, row, :]
            do = o[t] - (wide[X_WL] * se + wide[X_WR] * se_buf[t, after, :])
            woven[t, pl.ds(0, LANES, stride=2), :] = de
            woven[t, pl.ds(1, LANES, stride=2), :] = do
            detail[zi, :, part] = woven[t]
            de_buf[t, body, :] = de
            de_buf[t, pl.ds(7, 1), :] = rh[0, t, row, :]
            de_buf[t, pl.ds(8 + LANES, 1), :] = rh[3, t, row, :]
            do_buf[t, body, :] = do
            do_buf[t, pl.ds(7, 1), :] = rh[1, t, row, :] - wrm * se[0:1, :]
            load = (
                wide[X_K3] * de
                + wide[X_K4] * do
                + wide[X_K1] * de_buf[t, before, :]
                + wide[X_K2] * do_buf[t, before, :]
                + wide[X_K5] * de_buf[t, after, :]
            )
            hi, lo = split(load)
            high.append(hi)
            low.append(lo)
        coarse[zi] = jnp.where(
            lane < LANES // 2,
            jnp.take_along_axis(e[0], pick, axis=1, mode="promise_in_bounds"),
            jnp.take_along_axis(e[1], pick, axis=1, mode="promise_in_bounds"),
        )
        mine = (lane & (PLANES - 1)) == z
        high.append(jnp.where(mine, lch[...].astype(F32), 0.0).astype(BF16))
        low.append(jnp.where(mine, lcl[...].astype(F32), 0.0).astype(BF16))
        both = mxu(jnp.concatenate(high, axis=1), wcat[...])
        rest = mxu(jnp.concatenate(low, axis=1), wcat[:, 0:LANES])
        return both[:, :LANES] + both[:, LANES:] + rest

    for zi in range(0, STEP, 2):
        z = g * STEP + zi
        pair = jnp.concatenate([plane(zi, z), plane(zi + 1, z + 1)], axis=1)
        hi, lo = split(pair)
        solved = mxu(gxh[...], hi) + (mxu(gxh[...], lo) + mxu(gxl[...], hi))
        local[zi] = solved[:, :LANES]
        local[zi + 1] = solved[:, LANES:]


def exchange_kernel(
    nx, ny, local, colx, scal, cf, cb, out,
    xs, xr, ys, yr, sums, uwide, pwide, sx_sem, rx_sem, sy_sem, ry_sem,
):
    p, r = lax.axis_index("gx"), lax.axis_index("gy")
    barrier = pltpu.get_barrier_semaphore()
    for k in range(1, nx):
        pl.semaphore_signal(barrier, inc=1, device_id=(lax.rem(p + k, nx), r), device_id_type=MESH)
    for k in range(1, ny):
        pl.semaphore_signal(barrier, inc=1, device_id=(p, lax.rem(r + k, ny)), device_id_type=MESH)
    xs[0] = local[:, LANES - 1, :] * scal[S_FX : S_FX + 1, :]
    xs[1] = local[:, 0, :] * scal[S_BX : S_BX + 1, :]
    uwide[...] = column(colx[...], X_U)
    pwide[...] = column(colx[...], X_PSI)
    pl.semaphore_wait(barrier, nx + ny - 2)

    def start(sent, got, send_sem, recv_sem, own, count, target):
        copies = []
        for k in range(1, count):
            wraps = jnp.where(own + k >= count, 1, 0)
            copies.append(
                pltpu.make_async_remote_copy(
                    src_ref=sent.at[wraps], dst_ref=got.at[k - 1],
                    send_sem=send_sem.at[k - 1], recv_sem=recv_sem.at[k - 1],
                    device_id=target(lax.rem(own + k, count)), device_id_type=MESH,
                )
            )
            copies[-1].start()
        return copies

    def gather(copies, got, own, count, low):
        forward = jnp.zeros((PLANES, LANES), F32)
        backward = jnp.zeros((PLANES, LANES), F32)
        for k in range(1, count):
            copies[k - 1].wait()
            row = pl.ds(low + lax.rem(own + count - k, count), 1)
            values = got[k - 1]
            forward = forward + cf[row, :] * values
            backward = backward + cb[row, :] * values
        return forward, backward

    copies = start(xs, xr, sx_sem, rx_sem, p, nx, lambda i: (i, r))
    forward, backward = gather(copies, xr, p, nx, 0)
    sums[0] = forward
    sums[1] = backward
    lane = iota((PLANES, LANES), 1)
    blocks = LANES // PLANES

    def x_part(z, carry):
        last, head = carry
        row = pl.ds(z, 1)
        values = local[z] + uwide[...] * sums[0, row, :] + pwide[...] * sums[1, row, :]
        out[z] = values
        for m in range(blocks):
            block = values[m * PLANES : (m + 1) * PLANES, :]
            here = lane == m * PLANES + z
            last = jnp.where(here, block[:, LANES - 1 : LANES], last)
            head = jnp.where(here, block[:, 0:1], head)
        return last, head

    zero = jnp.zeros((PLANES, LANES), F32)
    last, head = lax.fori_loop(0, PLANES, x_part, (zero, zero), unroll=4)
    ys[0] = last * scal[S_FY : S_FY + 1, :]
    ys[1] = head * scal[S_BY : S_BY + 1, :]
    copies = start(ys, yr, sy_sem, ry_sem, r, ny, lambda j: (p, j))
    forward, backward = gather(copies, yr, r, ny, nx)
    sums[0] = forward
    sums[1] = backward
    u_y, psi_y = scal[S_UY : S_UY + 1, :], scal[S_PSIY : S_PSIY + 1, :]

    def y_part(z, carry):
        shift = lax.rem(LANES - z, LANES)
        f = pltpu.roll(sums[0], shift, 1)
        b = pltpu.roll(sums[1], shift, 1)
        for m in range(blocks):
            rows = pl.ds(m * PLANES, PLANES)
            at = m * PLANES
            out[z, rows, :] = out[z, rows, :] + (f[:, at : at + 1] * u_y + b[:, at : at + 1] * psi_y)
        return carry

    lax.fori_loop(0, PLANES, y_part, 0, unroll=4)


def per_device(nx, ny, density, spacing_x, spacing_y):
    blocks = nx + ny
    any_spec = pl.BlockSpec(memory_space=pl.ANY)
    vmem = pl.BlockSpec(memory_space=pltpu.VMEM)
    f32 = lambda *shape: jax.ShapeDtypeStruct(shape, F32)
    bf16 = lambda *shape: jax.ShapeDtypeStruct(shape, BF16)
    sx = spacing_x.reshape(2 * nx, LANES)
    sy = spacing_y.reshape(2 * ny, LANES)
    colx, ycoef, scal, cf, cb, wcat, gxh, gxl, rh, er, lch, lcl = pl.pallas_call(
        functools.partial(prepare_kernel, nx, ny),
        out_shape=(
            f32(LANES, LANES), f32(8, FINE), f32(8, LANES), f32(blocks, LANES), f32(blocks, LANES),
            bf16(FINE + LANES, FINE), bf16(LANES, LANES), bf16(LANES, LANES),
            f32(4, 2, PLANES, LANES), f32(LANES, LANES), bf16(LANES, LANES), bf16(LANES, LANES),
        ),
        in_specs=[any_spec, vmem, vmem],
        out_specs=(vmem,) * 12,
        scratch_shapes=[
            pltpu.VMEM((PLANES, FINE, FINE), F32),
            pltpu.VMEM((3, PLANES, FINE), F32),
            pltpu.VMEM((FINE, LANES), F32),
            pltpu.VMEM((3, PLANES, FINE), F32),
            pltpu.VMEM((FINE, LANES), F32),
            pltpu.VMEM((FINE, LANES), F32),
            pltpu.VMEM((6, 8, LANES), F32),
            pltpu.VMEM((14, blocks, LANES), F32),
            pltpu.VMEM((3, blocks, LANES), F32),
            pltpu.VMEM((LANES, LANES), F32),
            pltpu.VMEM((FINE, LANES), F32),
            pltpu.VMEM((FINE, LANES), F32),
            pltpu.SemaphoreType.DMA((PLANES // STEP,)),
            pltpu.SemaphoreType.DMA((10,)),
            pltpu.SemaphoreType.DMA((10,)),
        ],
        compiler_params=pltpu.CompilerParams(
            collective_id=0, has_side_effects=True, vmem_limit_bytes=32 * MIB
        ),
        name="prepare",
    )(density, sx, sy)
    whole = lambda array: pl.BlockSpec(array.shape, lambda g: (0,) * array.ndim, pipeline_mode=pl.Buffered(1))
    tables = (colx, ycoef, scal, rh, er, lch, lcl, wcat, gxh, gxl)
    detail, local, coarse = pl.pallas_call(
        main_kernel,
        grid=(PLANES // STEP,),
        out_shape=(f32(PLANES, FINE, FINE), f32(PLANES, LANES, LANES), f32(PLANES, LANES, LANES)),
        in_specs=[
            pl.BlockSpec((STEP, FINE, LANES), lambda g: (g, 0, 0)),
            pl.BlockSpec((STEP, FINE, LANES), lambda g: (g, 0, 1)),
        ]
        + [whole(t) for t in tables],
        out_specs=(
            pl.BlockSpec((STEP, FINE, FINE), lambda g: (g, 0, 0)),
            pl.BlockSpec((STEP, LANES, LANES), lambda g: (g, 0, 0)),
            pl.BlockSpec((STEP, LANES, LANES), lambda g: (g, 0, 0)),
        ),
        scratch_shapes=[
            pltpu.VMEM((7, LANES, LANES), F32),
            pltpu.VMEM((2, LANES + 16, LANES), F32),
            pltpu.VMEM((2, LANES + 16, LANES), F32),
            pltpu.VMEM((2, LANES + 16, LANES), F32),
            pltpu.VMEM((2, FINE, LANES), F32),
        ],
        compiler_params=pltpu.CompilerParams(vmem_limit_bytes=32 * MIB),
        name="main",
    )(density, density, *tables)
    correction = pl.pallas_call(
        functools.partial(exchange_kernel, nx, ny),
        out_shape=f32(PLANES, LANES, LANES),
        in_specs=[vmem] * 5,
        out_specs=vmem,
        scratch_shapes=[
            pltpu.VMEM((2, PLANES, LANES), F32),
            pltpu.VMEM((nx - 1, PLANES, LANES), F32),
            pltpu.VMEM((2, PLANES, LANES), F32),
            pltpu.VMEM((ny - 1, PLANES, LANES), F32),
            pltpu.VMEM((2, PLANES, LANES), F32),
            pltpu.VMEM((LANES, LANES), F32),
            pltpu.VMEM((LANES, LANES), F32),
            pltpu.SemaphoreType.DMA((nx - 1,)),
            pltpu.SemaphoreType.DMA((nx - 1,)),
            pltpu.SemaphoreType.DMA((ny - 1,)),
            pltpu.SemaphoreType.DMA((ny - 1,)),
        ],
        compiler_params=pltpu.CompilerParams(
            collective_id=1, has_side_effects=True, vmem_limit_bytes=32 * MIB
        ),
        name="exchange",
    )(local, colx, scal, cf, cb)
    return detail, coarse + correction


def solution(mesh):
    placed = P(None, "gx", "gy")
    return jax.shard_map(
        functools.partial(per_device, mesh.shape["gx"], mesh.shape["gy"]),
        mesh=mesh,
        in_specs=(placed, P(), P()),
        out_specs=(placed, placed),
        check_vma=False,
    )
```

profile of v0, /device:TPU:1, one launch (start us, length us, event | category | flops | bytes accessed | tf_op | source)
XLA Modules:
  0.0 54.9 jit_solution(15556031765451860134)
XLA Ops:
  0.6 0.0 copy-start
  0.6 3.4 %copy-done = f32[32,256,256]{2,1,0:T(8,128)S(1)} copy-done((f32[32,256,256]{2,1,0:T(8,128)S(1)}, f32[32,256,256]{2,1,0:T(8,128)}, u32[]{:S(2)}) %copy-start) | copy-done | bytes 8388632
  4.0 0.0 copy-start.1
  4.0 0.7 %copy-done.1 = f32[4096]{0:T(1024)S(1)} copy-done((f32[4096]{0:T(1024)S(1)}, f32[4096]{0:T(1024)}, u32[]{:S(2)}) %copy-start.1) | copy-done | bytes 16408
  4.7 0.0 copy-start.2
  4.7 0.7 %copy-done.2 = f32[2048]{0:T(1024)S(1)} copy-done((f32[2048]{0:T(1024)S(1)}, f32[2048]{0:T(1024)}, u32[]{:S(2)}) %copy-start.2) | copy-done | bytes 8216
  5.4 17.2 %prepare.1 = (f32[128,128]{1,0:T(8,128)S(1)}, f32[8,256]{1,0:T(8,128)S(1)}, f32[8,128]{1,0:T(8,128)S(1)}, f32[24,128]{1,0:T(8,128)S(1)}, f32[24,128]{1,0:T(8,128...) custom-call(f32[32,256,256]{2,1,0:T(8,128)S(1)} %copy-done, ...), custom_call_target="tpu_custom_call" | custom-call | tf_op jit(solution)/shard_map/prepare/pallas_call | solution.py:514
  22.6 12.1 %main.1 = (f32[32,256,256]{2,1,0:T(8,128)}, f32[32,128,128]{2,1,0:T(8,128)S(1)}, f32[32,128,128]{2,1,0:T(8,128)S(1)}) custom-call(f32[32,256,256]{2,1,0:T(8,128)S(1)} %copy-done, f32[32,256,256]{2,1,0:T(8,128)S(1)} %copy-done, f32[128,128]{1,0:T(8,128)S(1)} %get-tuple-element.17.colx, f32[8,256]{1,0:T(8,128)S(1)} %get-tuple-element.18.ycoef, ...), custom_call_target="tpu_custom_call" | custom-call | tf_op jit(solution)/shard_map/main/pallas_call | solution.py:547
  34.8 18.6 %exchange.1 = f32[32,128,128]{2,1,0:T(8,128)S(1)} custom-call(f32[32,128,128]{2,1,0:T(8,128)S(1)} %get-tuple-element.29.local, f32[128,128]{1,0:T(8,128)S(1)} %get-tuple-element.17.colx, f32[8,128]{1,0:T(8,128)S(1)} %get-tuple-element.19.scal, f32[24,128]{1,0:T(8,128)S(1)} %get-tuple-element.30.cf, f32[24,128]{1,0:T(8,128)S(1)} %get-tuple-element.31.cb), custom_call_target="tpu_custom_call" | custom-call | tf_op jit(solution)/shard_map/exchange/pallas_call | solution.py:571
  53.4 1.6 %add.3 = f32[32,128,128]{2,1,0:T(8,128)} add(f32[32,128,128]{2,1,0:T(8,128)S(1)} %get-tuple-element.28, f32[32,128,128]{2,1,0:T(8,128)S(1)} %exchange.1) | non-fusion elementwise | flops 524288 | bytes 6291456 | tf_op jit(solution)/shard_map/add | solution.py:594
Async XLA Ops:
  0.6 3.4 %copy-start = (f32[32,256,256]{2,1,0:T(8,128)S(1)}, f32[32,256,256]{2,1,0:T(8,128)}, u32[]{:S(2)}) copy-start(f32[32,256,256]{2,1,0:T(8,128)} %dens_r.1) | copy-start | bytes 25165828
  4.0 0.7 %copy-start.1 = (f32[4096]{0:T(1024)S(1)}, f32[4096]{0:T(1024)}, u32[]{:S(2)}) copy-start(f32[4096]{0:T(1024)} %param.5) | copy-start | bytes 49156
  4.7 0.7 %copy-start.2 = (f32[2048]{0:T(1024)S(1)}, f32[2048]{0:T(1024)}, u32[]{:S(2)}) copy-start(f32[2048]{0:T(1024)} %param.4) | copy-start | bytes 24580
where the time goes:
time: 55.5 us; the launch traced here: 54.9 us
  Pallas kernels  47.9 us (86%)
  local copies, waits for them, and re-layouts  4.79 us (9%)
  other arithmetic  1.57 us (3%)
  between operations  0.66 us (1%)
    pallas_call x1, Pallas kernels, per_device(): pl.pallas_call(functools.partial(exchange_kernel, nx, ny), out_shape=f32(...  18.6 us
    pallas_call x1, Pallas kernels, per_device(): pl.pallas_call(functools.partial(prepare_kernel, nx, ny), out_shape=(f32(...  17.2 us
    pallas_call x1, Pallas kernels, per_device(): pl.pallas_call(main_kernel, grid=(PLANES // STEP,), out_shape=(f32(PLANES...  12.1 us
    unnamed x6, local copies, waits for them, and re-layouts  4.79 us
    add x1, other arithmetic, per_device(): return (detail, coarse + correction)  1.57 us

commit v1 on v0

--- a/solution.py
+++ b/solution.py
@@ -157,9 +157,10 @@
 
 
 def prepare_kernel(
-    nx, ny, dens, sx, sy,
-    colx, ycoef, scal, cf, cb, wcat, gxh, gxl, rh, er, lch, lcl,
-    box, rsend, csend, rrecv, cl, cr, tiles, tab, rows_in, stack, wfine, merged, load_sem, send_sem, recv_sem,
+    nx, ny, dens, sx_in, sy_in,
+    colx, ycoef, scal, cf, cb, wcat, gxh, gxl, rh, er, lch, lcl, packed, box,
+    sx, sy, rsend, to_right, to_left, rrecv, from_left, from_right, tiles,
+    tab, rows_in, stack, wfine, load_sem, send_sem, recv_sem,
 ):
     p, r = lax.axis_index("gx"), lax.axis_index("gy")
     up, down = lax.rem(p + nx - 1, nx), lax.rem(p + 1, nx)
@@ -169,6 +170,9 @@
         part = pl.ds(k * STEP, STEP)
         loads.append(pltpu.make_async_copy(dens.at[part], box.at[part], load_sem.at[k]))
         loads[-1].start()
+    for k, (src, dst) in enumerate(((sx_in, sx), (sy_in, sy))):
+        loads.append(pltpu.make_async_copy(src, dst, load_sem.at[PLANES // STEP + k]))
+        loads[-1].start()
     barrier = pltpu.get_barrier_semaphore()
     for i in (up, p, down):
         for j in (left, r, right):
@@ -176,34 +180,43 @@
                 continue
             pl.semaphore_signal(barrier, inc=1, device_id=(i, j), device_id_type=MESH)
 
-    lane_f = iota((FINE, LANES), 1)
-    csend[...] = jnp.zeros((FINE, LANES), F32)
+    right_rows, left_rows = FINE // 2, FINE // 4
+    lane_r, lane_l = iota((right_rows, LANES), 1), iota((left_rows, LANES), 1)
+    to_right[...] = jnp.zeros((right_rows, LANES), F32)
+    to_left[...] = jnp.zeros((left_rows, LANES), F32)
     for k in range(PLANES // STEP):
         loads[k].wait()
-        acc = csend[...]
+        acc_r, acc_l = to_right[...], to_left[...]
         for zi in range(STEP):
             z = k * STEP + zi
-            acc = jnp.where(lane_f == z, box[z, :, FINE - 2 : FINE - 1], acc)
-            acc = jnp.where(lane_f == PLANES + z, box[z, :, FINE - 1 : FINE], acc)
-            acc = jnp.where(lane_f == 2 * PLANES + z, box[z, :, 0:1], acc)
+            for m in range(2):
+                rows = slice(m * right_rows, (m + 1) * right_rows)
+                at = 2 * m * PLANES + z
+                acc_r = jnp.where(lane_r == at, box[z, rows, FINE - 2 : FINE - 1], acc_r)
+                acc_r = jnp.where(lane_r == at + PLANES, box[z, rows, FINE - 1 : FINE], acc_r)
+            for m in range(4):
+                rows = slice(m * left_rows, (m + 1) * left_rows)
+                acc_l = jnp.where(lane_l == m * PLANES + z, box[z, rows, 0:1], acc_l)
             rsend[0, z : z + 1, :] = box[z, FINE - 2 : FINE - 1, :]
             rsend[1, z : z + 1, :] = box[z, FINE - 1 : FINE, :]
             rsend[2, z : z + 1, :] = box[z, 0:1, :]
-        csend[...] = acc
+        to_right[...] = acc_r
+        to_left[...] = acc_l
 
     pl.semaphore_wait(barrier, 8)
-    top, bottom = pl.ds(0, 8), pl.ds(FINE - 8, 8)
+    top = pl.ds(0, 8)
+    end_r, end_l = pl.ds(right_rows - 8, 8), pl.ds(left_rows - 8, 8)
     plan = (
+        (to_right, from_left, p, right),
+        (to_left, from_right, p, left),
         (rsend.at[pl.ds(0, 2)], rrecv.at[pl.ds(0, 2)], down, r),
         (rsend.at[pl.ds(2, 1)], rrecv.at[pl.ds(2, 1)], up, r),
-        (csend, cl, p, right),
-        (csend, cr, p, left),
-        (csend.at[bottom], tiles.at[0], down, r),
-        (csend.at[top], tiles.at[1], up, r),
-        (csend.at[bottom], tiles.at[2], down, right),
-        (csend.at[bottom], tiles.at[3], down, left),
-        (csend.at[top], tiles.at[4], up, right),
-        (csend.at[top], tiles.at[5], up, left),
+        (to_left.at[end_l], tiles.at[0], down, r),
+        (to_left.at[top], tiles.at[1], up, r),
+        (to_right.at[end_r], tiles.at[2], down, right),
+        (to_left.at[end_l], tiles.at[3], down, left),
+        (to_right.at[top], tiles.at[4], up, right),
+        (to_left.at[top], tiles.at[5], up, left),
     )
     copies = []
     for k, (src, dst, i, j) in enumerate(plan):
@@ -215,6 +228,8 @@
         )
         copies[-1].start()
 
+    for load in loads[PLANES // STEP :]:
+        load.wait()
     chain_tables(nx, ny, sx, sy, tab, rows_in)
     weights_between(tab[11], 0, nx, p, cf, cb)
     weights_between(tab[11], nx, ny, r, cf, cb)
@@ -245,6 +260,13 @@
     scal[S_UY : S_UY + 1, :] = uy
     scal[S_PSIY : S_PSIY + 1, :] = wy * tab[11, row_y, :]
 
+    lane_z = iota((PLANES, LANES), 1)
+    for k, index in enumerate((X_U, X_PSI)):
+        packed[k] = sum(
+            jnp.where(lane_z // PLANES == m, cols[m * PLANES : (m + 1) * PLANES, index : index + 1], 0.0)
+            for m in range(LANES // PLANES)
+        )
+
     odd_row = (iota((1, LANES), 1) & 1) == 1
     ycoef[...] = jnp.zeros((8, FINE), F32)
     for t in range(2):
@@ -282,16 +304,38 @@
     has_right = (r < ny - 1).astype(F32)
     lane_8 = iota((8, LANES), 1)
     lane = iota((LANES, LANES), 1)
-    merged[...] = jnp.where(lane_f < 2 * PLANES, cl[...] * has_left, cr[...] * has_right)
-    e_c, o_c = merged[pl.ds(0, LANES, stride=2), :], merged[pl.ds(1, LANES, stride=2), :]
-    own = csend[pl.ds(0, LANES, stride=2), :]
-    own_n, own_s = tiles[0] * has_up, tiles[1] * has_down
-    north = jnp.where(lane_8 < 2 * PLANES, tiles[2] * has_left, tiles[3] * has_right) * has_up
-    south = jnp.where(lane_8 < 2 * PLANES, tiles[4] * has_left, tiles[5] * has_right) * has_down
+
+    def unpack(ref, start, shifts):
+        values = ref[pl.ds(start, LANES // len(shifts), stride=2), :]
+        return jnp.concatenate([pltpu.roll(values, n, 1) if n else values for n in shifts], axis=0)
+
+    e_c, o_c = (
+        jnp.where(
+            lane < 2 * PLANES,
+            unpack(from_left, start, (0, 64)) * has_left,
+            unpack(from_right, start, (64, 32, 0, 96)) * has_right,
+        )
+        for start in range(2)
+    )
+    own = unpack(to_left, 0, (32, 0, 96, 64))
+    own_n = pltpu.roll(tiles[0], 64, 1) * has_up
+    own_s = pltpu.roll(tiles[1], 32, 1) * has_down
+    north = (
+        jnp.where(
+            lane_8 < 2 * PLANES,
+            pltpu.roll(tiles[2], 64, 1) * has_left,
+            pltpu.roll(tiles[3], 96, 1) * has_right,
+        )
+        * has_up
+    )
+    south = (
+        jnp.where(lane_8 < 2 * PLANES, tiles[4] * has_left, pltpu.roll(tiles[5], 64, 1) * has_right)
+        * has_down
+    )
 
     def along_y(values, own_values):
         at = iota(values.shape, 1)
-        guess = wl_y * pltpu.roll(values, PLANES, 1) + wr_y * pltpu.roll(own_values, LANES - PLANES, 1)
+        guess = wl_y * pltpu.roll(values, PLANES, 1) + wr_y * own_values
         return jnp.where((at >= PLANES) & (at < 2 * PLANES), guess, values)
 
     se = along_y(e_c, own)
@@ -319,7 +363,6 @@
     corner = stack[...].T
     corner_n = corner[2 * PLANES : 3 * PLANES, 6:7]
     corner_s = corner[2 * PLANES : 3 * PLANES, 8:9]
-    lane_z = iota((PLANES, LANES), 1)
     odd = (lane_z & 1) == 1
 
     def row_along_y(layer, scale, corner_col):
@@ -421,7 +464,7 @@
 
 
 def exchange_kernel(
-    nx, ny, local, colx, scal, cf, cb, out,
+    nx, ny, local, coarse, colx, scal, cf, cb, packed, mid, outer_l, outer_r,
     xs, xr, ys, yr, sums, uwide, pwide, sx_sem, rx_sem, sy_sem, ry_sem,
 ):
     p, r = lax.axis_index("gx"), lax.axis_index("gy")
@@ -454,86 +497,115 @@
         forward = jnp.zeros((PLANES, LANES), F32)
         backward = jnp.zeros((PLANES, LANES), F32)
         for k in range(1, count):
-            copies[k - 1].wait()
+            copies[k - 1].wait_recv()
             row = pl.ds(low + lax.rem(own + count - k, count), 1)
             values = got[k - 1]
             forward = forward + cf[row, :] * values
             backward = backward + cb[row, :] * values
         return forward, backward
 
-    copies = start(xs, xr, sx_sem, rx_sem, p, nx, lambda i: (i, r))
-    forward, backward = gather(copies, xr, p, nx, 0)
-    sums[0] = forward
-    sums[1] = backward
+    x_copies = start(xs, xr, sx_sem, rx_sem, p, nx, lambda i: (i, r))
+
     lane = iota((PLANES, LANES), 1)
     blocks = LANES // PLANES
 
-    def x_part(z, carry):
+    def edges(z, carry):
         last, head = carry
-        row = pl.ds(z, 1)
-        values = local[z] + uwide[...] * sums[0, row, :] + pwide[...] * sums[1, row, :]
-        out[z] = values
         for m in range(blocks):
-            block = values[m * PLANES : (m + 1) * PLANES, :]
+            block = local[z, pl.ds(m * PLANES, PLANES), :]
             here = lane == m * PLANES + z
             last = jnp.where(here, block[:, LANES - 1 : LANES], last)
             head = jnp.where(here, block[:, 0:1], head)
         return last, head
 
     zero = jnp.zeros((PLANES, LANES), F32)
-    last, head = lax.fori_loop(0, PLANES, x_part, (zero, zero), unroll=4)
-    ys[0] = last * scal[S_FY : S_FY + 1, :]
-    ys[1] = head * scal[S_BY : S_BY + 1, :]
-    copies = start(ys, yr, sy_sem, ry_sem, r, ny, lambda j: (p, j))
-    forward, backward = gather(copies, yr, r, ny, nx)
+    last, head = lax.fori_loop(0, PLANES, edges, (zero, zero), unroll=4)
+    forward, backward = gather(x_copies, xr, p, nx, 0)
     sums[0] = forward
     sums[1] = backward
-    u_y, psi_y = scal[S_UY : S_UY + 1, :], scal[S_PSIY : S_PSIY + 1, :]
-
-    def y_part(z, carry):
-        shift = lax.rem(LANES - z, LANES)
-        f = pltpu.roll(sums[0], shift, 1)
-        b = pltpu.roll(sums[1], shift, 1)
-        for m in range(blocks):
-            rows = pl.ds(m * PLANES, PLANES)
-            at = m * PLANES
-            out[z, rows, :] = out[z, rows, :] + (f[:, at : at + 1] * u_y + b[:, at : at + 1] * psi_y)
+    across_f = jnp.concatenate([forward] * blocks, axis=0).T
+    across_b = jnp.concatenate([backward] * blocks, axis=0).T
+    u_x, psi_x = packed[0], packed[1]
+    end = slice(LANES - 1, LANES)
+    ys[0] = (last + u_x * across_f[end, :] + psi_x * across_b[end, :]) * scal[S_FY : S_FY + 1, :]
+    ys[1] = (head + u_x * across_f[0:1, :] + psi_x * across_b[0:1, :]) * scal[S_BY : S_BY + 1, :]
+    y_copies = start(ys, yr, sy_sem, ry_sem, r, ny, lambda j: (p, j))
+
+    edge = jnp.where(
+        (iota((LANES, LANES), 0) // PLANES) % 2 == 0,
+        scal[S_UY : S_UY + 1, :], scal[S_PSIY : S_PSIY + 1, :],
+    )
+    edge_h = edge.astype(BF16).astype(F32)
+    edge_l = edge - edge_h
+    plane_of = iota((LANES, LANES), 0) % PLANES
+
+    def x_part(z, carry):
+        row = pl.ds(z, 1)
+        mid[z] = local[z] + coarse[z] + uwide[...] * sums[0, row, :] + pwide[...] * sums[1, row, :]
+        outer_r[z, 0:LANES, :] = jnp.where(plane_of == z, edge_h, 0.0).astype(BF16)
+        outer_r[z, LANES:, :] = jnp.where(plane_of == z, edge_l, 0.0).astype(BF16)
         return carry
 
-    lax.fori_loop(0, PLANES, y_part, 0, unroll=4)
+    lax.fori_loop(0, PLANES, x_part, 0, unroll=2)
+    forward, backward = gather(y_copies, yr, r, ny, nx)
+    lane = iota((LANES, LANES), 1)
+
+    def spread(values):
+        return jnp.concatenate(
+            [pltpu.roll(values, (LANES - m * PLANES) % LANES, 1) if m else values for m in range(blocks)],
+            axis=0,
+        )
+
+    both = jnp.where(lane < PLANES, spread(forward), pltpu.roll(spread(backward), PLANES, 1))
+    high = both.astype(BF16).astype(F32)
+    both = jnp.where(lane < 2 * PLANES, high, pltpu.roll(both - high, 2 * PLANES, 1))
+    outer_l[:, 0:LANES] = both.astype(BF16)
+    outer_l[:, LANES:] = both.astype(BF16)
+    for copy in x_copies + y_copies:
+        copy.wait_send()
+
+
+def final_kernel(mid, outer_l, outer_r, out):
+    for z in range(0, mid.shape[0], 2):
+        pair = jnp.concatenate([outer_r[z], outer_r[z + 1]], axis=1)
+        update = mxu(outer_l[...], pair)
+        out[z] = mid[z] + update[:, :LANES]
+        out[z + 1] = mid[z + 1] + update[:, LANES:]
 
 
 def per_device(nx, ny, density, spacing_x, spacing_y):
     blocks = nx + ny
-    any_spec = pl.BlockSpec(memory_space=pl.ANY)
+    hbm = pl.BlockSpec(memory_space=pltpu.HBM)
     vmem = pl.BlockSpec(memory_space=pltpu.VMEM)
     f32 = lambda *shape: jax.ShapeDtypeStruct(shape, F32)
     bf16 = lambda *shape: jax.ShapeDtypeStruct(shape, BF16)
     sx = spacing_x.reshape(2 * nx, LANES)
     sy = spacing_y.reshape(2 * ny, LANES)
-    colx, ycoef, scal, cf, cb, wcat, gxh, gxl, rh, er, lch, lcl = pl.pallas_call(
+    colx, ycoef, scal, cf, cb, wcat, gxh, gxl, rh, er, lch, lcl, packed, box = pl.pallas_call(
         functools.partial(prepare_kernel, nx, ny),
         out_shape=(
             f32(LANES, LANES), f32(8, FINE), f32(8, LANES), f32(blocks, LANES), f32(blocks, LANES),
             bf16(FINE + LANES, FINE), bf16(LANES, LANES), bf16(LANES, LANES),
             f32(4, 2, PLANES, LANES), f32(LANES, LANES), bf16(LANES, LANES), bf16(LANES, LANES),
+            f32(2, PLANES, LANES), f32(PLANES, FINE, FINE),
         ),
-        in_specs=[any_spec, vmem, vmem],
-        out_specs=(vmem,) * 12,
+        in_specs=[hbm] * 3,
+        out_specs=(vmem,) * 14,
         scratch_shapes=[
-            pltpu.VMEM((PLANES, FINE, FINE), F32),
+            pltpu.VMEM((2 * nx, LANES), F32),
+            pltpu.VMEM((2 * ny, LANES), F32),
             pltpu.VMEM((3, PLANES, FINE), F32),
-            pltpu.VMEM((FINE, LANES), F32),
+            pltpu.VMEM((FINE // 2, LANES), F32),
+            pltpu.VMEM((FINE // 4, LANES), F32),
             pltpu.VMEM((3, PLANES, FINE), F32),
-            pltpu.VMEM((FINE, LANES), F32),
-            pltpu.VMEM((FINE, LANES), F32),
+            pltpu.VMEM((FINE // 2, LANES), F32),
+            pltpu.VMEM((FINE // 4, LANES), F32),
             pltpu.VMEM((6, 8, LANES), F32),
             pltpu.VMEM((14, blocks, LANES), F32),
             pltpu.VMEM((3, blocks, LANES), F32),
             pltpu.VMEM((LANES, LANES), F32),
             pltpu.VMEM((FINE, LANES), F32),
-            pltpu.VMEM((FINE, LANES), F32),
-            pltpu.SemaphoreType.DMA((PLANES // STEP,)),
+            pltpu.SemaphoreType.DMA((PLANES // STEP + 2,)),
             pltpu.SemaphoreType.DMA((10,)),
             pltpu.SemaphoreType.DMA((10,)),
         ],
@@ -541,7 +613,7 @@
             collective_id=0, has_side_effects=True, vmem_limit_bytes=32 * MIB
         ),
         name="prepare",
-    )(density, sx, sy)
+    )(*(pltpu.with_memory_space_constraint(v, pltpu.HBM) for v in (density, sx, sy)))
     whole = lambda array: pl.BlockSpec(array.shape, lambda g: (0,) * array.ndim, pipeline_mode=pl.Buffered(1))
     tables = (colx, ycoef, scal, rh, er, lch, lcl, wcat, gxh, gxl)
     detail, local, coarse = pl.pallas_call(
@@ -567,12 +639,12 @@
         ],
         compiler_params=pltpu.CompilerParams(vmem_limit_bytes=32 * MIB),
         name="main",
-    )(density, density, *tables)
-    correction = pl.pallas_call(
+    )(box, box, *tables)
+    mid, outer_l, outer_r = pl.pallas_call(
         functools.partial(exchange_kernel, nx, ny),
-        out_shape=f32(PLANES, LANES, LANES),
-        in_specs=[vmem] * 5,
-        out_specs=vmem,
+        out_shape=(f32(PLANES, LANES, LANES), bf16(LANES, FINE), bf16(PLANES, FINE, LANES)),
+        in_specs=[vmem] * 7,
+        out_specs=(vmem,) * 3,
         scratch_shapes=[
             pltpu.VMEM((2, PLANES, LANES), F32),
             pltpu.VMEM((nx - 1, PLANES, LANES), F32),
@@ -590,8 +662,21 @@
             collective_id=1, has_side_effects=True, vmem_limit_bytes=32 * MIB
         ),
         name="exchange",
-    )(local, colx, scal, cf, cb)
-    return detail, coarse + correction
+    )(local, coarse, colx, scal, cf, cb, packed)
+    coarse_new = pl.pallas_call(
+        final_kernel,
+        grid=(PLANES // 8,),
+        out_shape=f32(PLANES, LANES, LANES),
+        in_specs=[
+            pl.BlockSpec((8, LANES, LANES), lambda g: (g, 0, 0)),
+            pl.BlockSpec((LANES, FINE), lambda g: (0, 0)),
+            pl.BlockSpec((8, FINE, LANES), lambda g: (g, 0, 0)),
+        ],
+        out_specs=pl.BlockSpec((8, LANES, LANES), lambda g: (g, 0, 0)),
+        compiler_params=pltpu.CompilerParams(vmem_limit_bytes=32 * MIB),
+        name="final",
+    )(mid, outer_l, outer_r)
+    return detail, coarse_new
 
 
 def solution(mesh):

time: 55.5 us -> 45.1 us (0.81)
  local copies, waits for them, and re-layouts: 4.79 us -> 0 us
  Pallas kernels: 47.9 us -> 44.1 us
  other arithmetic: 1.57 us -> 0 us
    unnamed x6 -> x0, local copies, waits for them, and re-layouts: 4.79 us -> none
    pallas_call x1 -> x2, Pallas kernels: 18.6 us -> 15.2 us  [the longest x1 12.9 us: per_device(): pl.pallas_call(functools.partial(exchange_kernel, nx, ny), out_shape=(f32...]
    add x1 -> x0, other arithmetic: 1.57 us -> none  [per_device(): return (detail, coarse + correction)]
where the time goes in v1:
time: 45.1 us; the launch traced here: 44.7 us
  Pallas kernels  44.1 us (98%)
  between operations  0.65 us (1%)
    pallas_call x1, Pallas kernels, per_device(): pl.pallas_call(functools.partial(prepare_kernel, nx, ny), out_shape=(f32(...  16.8 us
    pallas_call x1, Pallas kernels, per_device(): pl.pallas_call(functools.partial(exchange_kernel, nx, ny), out_shape=(f32...  12.9 us
    pallas_call x1, Pallas kernels, per_device(): pl.pallas_call(main_kernel, grid=(PLANES // STEP,), out_shape=(f32(PLANES...  12.1 us
    pallas_call x1, Pallas kernels, per_device(): pl.pallas_call(final_kernel, grid=(PLANES // 8,), out_shape=f32(PLANES, L...  2.34 us

profile of v1, /device:TPU:1, one launch (start us, length us, event | category | flops | bytes accessed | tf_op | source)
XLA Modules:
  0.0 44.7 jit_solution(12860275304452265513)
XLA Ops:
  0.6 16.8 %prepare.1 = (f32[128,128]{1,0:T(8,128)S(1)}, f32[8,256]{1,0:T(8,128)S(1)}, f32[8,128]{1,0:T(8,128)S(1)}, f32[24,128]{1,0:T(8,128)S(1)}, f32[24,128]{1,0:T(8,128...) custom-call(f32[32,256,256]{2,1,0:T(8,128)} %dens.1, ...), custom_call_target="tpu_custom_call" | custom-call | tf_op jit(solution)/shard_map/prepare/pallas_call | solution.py:584
  17.4 12.1 %main.1 = (f32[32,256,256]{2,1,0:T(8,128)}, f32[32,128,128]{2,1,0:T(8,128)S(1)}, f32[32,128,128]{2,1,0:T(8,128)S(1)}) custom-call(f32[32,256,256]{2,1,0:T(8,128)S(1)} %get-tuple-element.22.dens_l.dens_r, f32[32,256,256]{2,1,0:T(8,128)S(1)} %get-tuple-element.22.dens_l.dens_r, f32[128,128]{1,0:T(8,128)S(1)} %get-tuple-element.23.colx, ...), custom_call_target="tpu_custom_call" | custom-call | tf_op jit(solution)/shard_map/main/pallas_call | solution.py:619
  29.5 12.9 %exchange.1 = (f32[32,128,128]{2,1,0:T(8,128)S(1)}, bf16[128,256]{1,0:T(8,128)(2,1)S(1)}, bf16[32,256,128]{2,1,0:T(8,128)(2,1)S(1)}) custom-call(f32[32,128,128]{2,1,0:T(8,128)S(1)} %get-tuple-element.34.local, f32[32,128,128]{2,1,0:T(8,128)S(1)} %get-tuple-element.35.coarse, f32[128,128]{1,0:T(8,128)S(1)} %get-tuple-element.23.colx, ...), custom_call_target="tpu_custom_call" | custom-call | tf_op jit(solution)/shard_map/exchange/pallas_call | solution.py:643
  42.4 2.3 %final.1 = f32[32,128,128]{2,1,0:T(8,128)} custom-call(f32[32,128,128]{2,1,0:T(8,128)S(1)} %get-tuple-element.39.mid, bf16[128,256]{1,0:T(8,128)(2,1)S(1)} %get-tuple-element.40.outer_l, bf16[32,256,128]{2,1,0:T(8,128)(2,1)S(1)} %get-tuple-element.41.outer_r), custom_call_target="tpu_custom_call" | custom-call | tf_op jit(solution)/shard_map/final/pallas_call | solution.py:666

commit v2 on v1

--- a/solution.py
+++ b/solution.py
@@ -16,6 +16,7 @@
 LANES = 128
 FINE = 256
 PLANES = 32
+PER = 8
 STEP = 4
 MIB = 1 << 20
 X_WL, X_WR, X_K1, X_K2, X_K3, X_K4, X_K5, X_U, X_PSI, X_W = range(10)
@@ -168,10 +169,15 @@
     loads = []
     for k in range(PLANES // STEP):
         part = pl.ds(k * STEP, STEP)
-        loads.append(pltpu.make_async_copy(dens.at[part], box.at[part], load_sem.at[k]))
-        loads[-1].start()
+        for t in range(2):
+            loads.append(
+                pltpu.make_async_copy(
+                    dens.at[part, :, pl.ds(t * LANES, LANES)], box.at[t, part], load_sem.at[2 * k + t]
+                )
+            )
+            loads[-1].start()
     for k, (src, dst) in enumerate(((sx_in, sx), (sy_in, sy))):
-        loads.append(pltpu.make_async_copy(src, dst, load_sem.at[PLANES // STEP + k]))
+        loads.append(pltpu.make_async_copy(src, dst, load_sem.at[2 * PLANES // STEP + k]))
         loads[-1].start()
     barrier = pltpu.get_barrier_semaphore()
     for i in (up, p, down):
@@ -185,21 +191,23 @@
     to_right[...] = jnp.zeros((right_rows, LANES), F32)
     to_left[...] = jnp.zeros((left_rows, LANES), F32)
     for k in range(PLANES // STEP):
-        loads[k].wait()
+        loads[2 * k].wait()
+        loads[2 * k + 1].wait()
         acc_r, acc_l = to_right[...], to_left[...]
         for zi in range(STEP):
             z = k * STEP + zi
             for m in range(2):
                 rows = slice(m * right_rows, (m + 1) * right_rows)
                 at = 2 * m * PLANES + z
-                acc_r = jnp.where(lane_r == at, box[z, rows, FINE - 2 : FINE - 1], acc_r)
-                acc_r = jnp.where(lane_r == at + PLANES, box[z, rows, FINE - 1 : FINE], acc_r)
+                acc_r = jnp.where(lane_r == at, box[1, z, rows, LANES - 2 : LANES - 1], acc_r)
+                acc_r = jnp.where(lane_r == at + PLANES, box[1, z, rows, LANES - 1 : LANES], acc_r)
             for m in range(4):
                 rows = slice(m * left_rows, (m + 1) * left_rows)
-                acc_l = jnp.where(lane_l == m * PLANES + z, box[z, rows, 0:1], acc_l)
-            rsend[0, z : z + 1, :] = box[z, FINE - 2 : FINE - 1, :]
-            rsend[1, z : z + 1, :] = box[z, FINE - 1 : FINE, :]
-            rsend[2, z : z + 1, :] = box[z, 0:1, :]
+                acc_l = jnp.where(lane_l == m * PLANES + z, box[0, z, rows, 0:1], acc_l)
+            for t in range(2):
+                rsend[0, t, z : z + 1, :] = box[t, z, FINE - 2 : FINE - 1, :]
+                rsend[1, t, z : z + 1, :] = box[t, z, FINE - 1 : FINE, :]
+                rsend[2, t, z : z + 1, :] = box[t, z, 0:1, :]
         to_right[...] = acc_r
         to_left[...] = acc_l
 
@@ -228,7 +236,7 @@
         )
         copies[-1].start()
 
-    for load in loads[PLANES // STEP :]:
+    for load in loads[2 * PLANES // STEP :]:
         load.wait()
     chain_tables(nx, ny, sx, sy, tab, rows_in)
     weights_between(tab[11], 0, nx, p, cf, cb)
@@ -366,7 +374,7 @@
     odd = (lane_z & 1) == 1
 
     def row_along_y(layer, scale, corner_col):
-        tiles_in = [layer[:, t * LANES : (t + 1) * LANES] * scale for t in range(2)]
+        tiles_in = [layer[t] * scale for t in range(2)]
         next_in = [pltpu.roll(v, LANES - 1, 1) for v in tiles_in]
         after = [
             jnp.where(lane_z < LANES - 1, next_in[0], next_in[1]),
@@ -382,90 +390,121 @@
     e_n, s_n = row_along_y(rrecv[0], has_up, corner_n)
     e_s, s_s = row_along_y(rrecv[2], has_down, corner_s)
     for t in range(2):
-        part = slice(t * LANES, (t + 1) * LANES)
         rh[0, t] = e_n[t] - s_n[t]
-        rh[1, t] = rrecv[1, :, part] * has_up - wl_x * s_n[t]
+        rh[1, t] = rrecv[1, t] * has_up - wl_x * s_n[t]
         rh[2, t] = s_s[t]
         rh[3, t] = e_s[t] - s_s[t]
 
 
 def main_kernel(
-    dens_l, dens_r, colx, ycoef, scal, rh, er, lch, lcl, wcat, gxh, gxl,
-    detail, local, coarse, wide, se_buf, de_buf, do_buf, woven,
+    box, colx, ycoef, scal, rh, er, lch, lcl, wcat, gxh, gxl,
+    detail, local, coarse, wide, se_buf, de_buf, do_buf, woven, high, low, sem,
 ):
-    g = pl.program_id(0)
-
-    @pl.when(g == 0)
-    def _():
-        for k in range(7):
-            wide[k] = column(colx[...], k)
-
+    for k in range(7):
+        wide[k] = column(colx[...], k)
     lane = iota((LANES, LANES), 1)
     odd = (lane & 1) == 1
     inner = lane < LANES - 1
     pick = (2 * lane) & (LANES - 1)
     wrm = scal[S_WRM : S_WRM + 1, :]
     body, before, after = pl.ds(8, LANES), pl.ds(7, LANES), pl.ds(9, LANES)
-
-    def plane(zi, z):
+    turns = PLANES // PER
+
+    def stencil(z, k, slot):
         row = pl.ds(z, 1)
-        parts = [slice(t * LANES, (t + 1) * LANES) for t in range(2)]
-        e = [dens[zi, pl.ds(0, LANES, stride=2), :] for dens in (dens_l, dens_r)]
-        o = [dens[zi, pl.ds(1, LANES, stride=2), :] for dens in (dens_l, dens_r)]
+        e = [box[t, z, pl.ds(0, LANES, stride=2), :] for t in range(2)]
+        o = [box[t, z, pl.ds(1, LANES, stride=2), :] for t in range(2)]
         nxt = [pltpu.roll(v, LANES - 1, 1) for v in e]
         beyond = pltpu.roll(er[...], lax.rem(3 * LANES - 1 - 2 * PLANES - z, LANES), 1)
         nxt = [jnp.where(inner, nxt[0], nxt[1]), jnp.where(inner, nxt[1], beyond)]
-        high, low = [], []
         for t in range(2):
-            part = parts[t]
+            part = slice(t * LANES, (t + 1) * LANES)
             guess = ycoef[0:1, part] * pltpu.roll(e[t], 1, 1) + ycoef[1:2, part] * nxt[t]
             se = jnp.where(odd, guess, e[t])
             de = e[t] - se
-            se_buf[t, body, :] = se
-            se_buf[t, pl.ds(8 + LANES, 1), :] = rh[2, t, row, :]
-            do = o[t] - (wide[X_WL] * se + wide[X_WR] * se_buf[t, after, :])
-            woven[t, pl.ds(0, LANES, stride=2), :] = de
-            woven[t, pl.ds(1, LANES, stride=2), :] = do
-            detail[zi, :, part] = woven[t]
-            de_buf[t, body, :] = de
-            de_buf[t, pl.ds(7, 1), :] = rh[0, t, row, :]
-            de_buf[t, pl.ds(8 + LANES, 1), :] = rh[3, t, row, :]
-            do_buf[t, body, :] = do
-            do_buf[t, pl.ds(7, 1), :] = rh[1, t, row, :] - wrm * se[0:1, :]
+            se_buf[k, t, body, :] = se
+            se_buf[k, t, pl.ds(8 + LANES, 1), :] = rh[2, t, row, :]
+            do = o[t] - (wide[X_WL] * se + wide[X_WR] * se_buf[k, t, after, :])
+            woven[slot, k, t, pl.ds(0, LANES, stride=2), :] = de
+            woven[slot, k, t, pl.ds(1, LANES, stride=2), :] = do
+            de_buf[k, t, body, :] = de
+            de_buf[k, t, pl.ds(7, 1), :] = rh[0, t, row, :]
+            de_buf[k, t, pl.ds(8 + LANES, 1), :] = rh[3, t, row, :]
+            do_buf[k, t, body, :] = do
+            do_buf[k, t, pl.ds(7, 1), :] = rh[1, t, row, :] - wrm * se[0:1, :]
             load = (
                 wide[X_K3] * de
                 + wide[X_K4] * do
-                + wide[X_K1] * de_buf[t, before, :]
-                + wide[X_K2] * do_buf[t, before, :]
-                + wide[X_K5] * de_buf[t, after, :]
+                + wide[X_K1] * de_buf[k, t, before, :]
+                + wide[X_K2] * do_buf[k, t, before, :]
+                + wide[X_K5] * de_buf[k, t, after, :]
             )
             hi, lo = split(load)
-            high.append(hi)
-            low.append(lo)
-        coarse[zi] = jnp.where(
+            high[slot, k, :, part] = hi
+            low[slot, k, :, part] = lo
+        coarse[z] = jnp.where(
             lane < LANES // 2,
             jnp.take_along_axis(e[0], pick, axis=1, mode="promise_in_bounds"),
             jnp.take_along_axis(e[1], pick, axis=1, mode="promise_in_bounds"),
         )
         mine = (lane & (PLANES - 1)) == z
-        high.append(jnp.where(mine, lch[...].astype(F32), 0.0).astype(BF16))
-        low.append(jnp.where(mine, lcl[...].astype(F32), 0.0).astype(BF16))
-        both = mxu(jnp.concatenate(high, axis=1), wcat[...])
-        rest = mxu(jnp.concatenate(low, axis=1), wcat[:, 0:LANES])
-        return both[:, :LANES] + both[:, LANES:] + rest
-
-    for zi in range(0, STEP, 2):
-        z = g * STEP + zi
-        pair = jnp.concatenate([plane(zi, z), plane(zi + 1, z + 1)], axis=1)
-        hi, lo = split(pair)
-        solved = mxu(gxh[...], hi) + (mxu(gxh[...], lo) + mxu(gxl[...], hi))
-        local[zi] = solved[:, :LANES]
-        local[zi + 1] = solved[:, LANES:]
+        high[slot, k, :, FINE:] = jnp.where(mine, lch[...].astype(F32), 0.0).astype(BF16)
+        low[slot, k, :, FINE:] = jnp.where(mine, lcl[...].astype(F32), 0.0).astype(BF16)
+
+    def solve(z, slot):
+        pairs = []
+        for k in range(0, PER, 2):
+            pair = []
+            for n in (k, k + 1):
+                both = mxu(high[slot, n], wcat[...])
+                rest = mxu(low[slot, n], wcat[:, 0:LANES])
+                pair.append(both[:, :LANES] + both[:, LANES:] + rest)
+            pairs.append(jnp.concatenate(pair, axis=1))
+        for k in range(0, PER, 2):
+            hi, lo = split(pairs[k // 2])
+            solved = mxu(gxh[...], hi) + (mxu(gxh[...], lo) + mxu(gxl[...], hi))
+            local[z + k] = solved[:, :LANES]
+            local[z + k + 1] = solved[:, LANES:]
+
+    def writes(it, slot):
+        return [
+            pltpu.make_async_copy(
+                woven.at[slot, :, t],
+                detail.at[pl.ds(PER * it, PER), :, pl.ds(t * LANES, LANES)],
+                sem.at[slot, t],
+            )
+            for t in range(2)
+        ]
+
+    def step(it, carry):
+        slot = lax.rem(it, 2)
+
+        @pl.when(it >= 2)
+        def _():
+            for write in writes(it - 2, slot):
+                write.wait()
+
+        solve(PER * it - PER, 1 - slot)
+        for k in range(PER):
+            stencil(PER * it + k, k, slot)
+        for write in writes(it, slot):
+            write.start()
+        return carry
+
+    for k in range(PER):
+        stencil(k, k, 0)
+    for write in writes(0, 0):
+        write.start()
+    lax.fori_loop(1, turns, step, 0)
+    solve(PLANES - PER, (turns - 1) % 2)
+    for it in (turns - 2, turns - 1):
+        for write in writes(it, it % 2):
+            write.wait()
 
 
 def exchange_kernel(
     nx, ny, local, coarse, colx, scal, cf, cb, packed, mid, outer_l, outer_r,
-    xs, xr, ys, yr, sums, uwide, pwide, sx_sem, rx_sem, sy_sem, ry_sem,
+    xs, xr, ys, yr, cs, cr, sums, uwide, pwide, sx_sem, rx_sem, sy_sem, ry_sem, sc_sem, rc_sem,
 ):
     p, r = lax.axis_index("gx"), lax.axis_index("gy")
     barrier = pltpu.get_barrier_semaphore()
@@ -477,7 +516,6 @@
     xs[1] = local[:, 0, :] * scal[S_BX : S_BX + 1, :]
     uwide[...] = column(colx[...], X_U)
     pwide[...] = column(colx[...], X_PSI)
-    pl.semaphore_wait(barrier, nx + ny - 2)
 
     def start(sent, got, send_sem, recv_sem, own, count, target):
         copies = []
@@ -494,8 +532,7 @@
         return copies
 
     def gather(copies, got, own, count, low):
-        forward = jnp.zeros((PLANES, LANES), F32)
-        backward = jnp.zeros((PLANES, LANES), F32)
+        forward = backward = 0.0
         for k in range(1, count):
             copies[k - 1].wait_recv()
             row = pl.ds(low + lax.rem(own + count - k, count), 1)
@@ -503,8 +540,6 @@
             forward = forward + cf[row, :] * values
             backward = backward + cb[row, :] * values
         return forward, backward
-
-    x_copies = start(xs, xr, sx_sem, rx_sem, p, nx, lambda i: (i, r))
 
     lane = iota((PLANES, LANES), 1)
     blocks = LANES // PLANES
@@ -520,16 +555,25 @@
 
     zero = jnp.zeros((PLANES, LANES), F32)
     last, head = lax.fori_loop(0, PLANES, edges, (zero, zero), unroll=4)
+    scale_f, scale_b = scal[S_FY : S_FY + 1, :], scal[S_BY : S_BY + 1, :]
+    ys[0] = last * scale_f
+    ys[1] = head * scale_b
+    pl.semaphore_wait(barrier, nx + ny - 2)
+    x_copies = start(xs, xr, sx_sem, rx_sem, p, nx, lambda i: (i, r))
+    y_copies = start(ys, yr, sy_sem, ry_sem, r, ny, lambda j: (p, j))
+
     forward, backward = gather(x_copies, xr, p, nx, 0)
     sums[0] = forward
     sums[1] = backward
     across_f = jnp.concatenate([forward] * blocks, axis=0).T
     across_b = jnp.concatenate([backward] * blocks, axis=0).T
-    u_x, psi_x = packed[0], packed[1]
     end = slice(LANES - 1, LANES)
-    ys[0] = (last + u_x * across_f[end, :] + psi_x * across_b[end, :]) * scal[S_FY : S_FY + 1, :]
-    ys[1] = (head + u_x * across_f[0:1, :] + psi_x * across_b[0:1, :]) * scal[S_BY : S_BY + 1, :]
-    y_copies = start(ys, yr, sy_sem, ry_sem, r, ny, lambda j: (p, j))
+    cs[...] = jnp.zeros((2, 8, LANES), F32)
+    cs[0, 0:1, :] = across_f[end, :] * scale_f
+    cs[0, 1:2, :] = across_b[end, :] * scale_f
+    cs[1, 0:1, :] = across_f[0:1, :] * scale_b
+    cs[1, 1:2, :] = across_b[0:1, :] * scale_b
+    c_copies = start(cs, cr, sc_sem, rc_sem, r, ny, lambda j: (p, j))
 
     edge = jnp.where(
         (iota((LANES, LANES), 0) // PLANES) % 2 == 0,
@@ -547,7 +591,11 @@
         return carry
 
     lax.fori_loop(0, PLANES, x_part, 0, unroll=2)
+    u_x, psi_x = packed[0], packed[1]
     forward, backward = gather(y_copies, yr, r, ny, nx)
+    extra_f, extra_b = gather(c_copies, cr, r, ny, nx)
+    forward = forward + u_x * extra_f[0:1, :] + psi_x * extra_f[1:2, :]
+    backward = backward + u_x * extra_b[0:1, :] + psi_x * extra_b[1:2, :]
     lane = iota((LANES, LANES), 1)
 
     def spread(values):
@@ -561,7 +609,7 @@
     both = jnp.where(lane < 2 * PLANES, high, pltpu.roll(both - high, 2 * PLANES, 1))
     outer_l[:, 0:LANES] = both.astype(BF16)
     outer_l[:, LANES:] = both.astype(BF16)
-    for copy in x_copies + y_copies:
+    for copy in x_copies + y_copies + c_copies:
         copy.wait_send()
 
 
@@ -587,17 +635,17 @@
             f32(LANES, LANES), f32(8, FINE), f32(8, LANES), f32(blocks, LANES), f32(blocks, LANES),
             bf16(FINE + LANES, FINE), bf16(LANES, LANES), bf16(LANES, LANES),
             f32(4, 2, PLANES, LANES), f32(LANES, LANES), bf16(LANES, LANES), bf16(LANES, LANES),
-            f32(2, PLANES, LANES), f32(PLANES, FINE, FINE),
+            f32(2, PLANES, LANES), f32(2, PLANES, FINE, LANES),
         ),
         in_specs=[hbm] * 3,
         out_specs=(vmem,) * 14,
         scratch_shapes=[
             pltpu.VMEM((2 * nx, LANES), F32),
             pltpu.VMEM((2 * ny, LANES), F32),
-            pltpu.VMEM((3, PLANES, FINE), F32),
+            pltpu.VMEM((3, 2, PLANES, LANES), F32),
             pltpu.VMEM((FINE // 2, LANES), F32),
             pltpu.VMEM((FINE // 4, LANES), F32),
-            pltpu.VMEM((3, PLANES, FINE), F32),
+            pltpu.VMEM((3, 2, PLANES, LANES), F32),
             pltpu.VMEM((FINE // 2, LANES), F32),
             pltpu.VMEM((FINE // 4, LANES), F32),
             pltpu.VMEM((6, 8, LANES), F32),
@@ -605,7 +653,7 @@
             pltpu.VMEM((3, blocks, LANES), F32),
             pltpu.VMEM((LANES, LANES), F32),
             pltpu.VMEM((FINE, LANES), F32),
-            pltpu.SemaphoreType.DMA((PLANES // STEP + 2,)),
+            pltpu.SemaphoreType.DMA((2 * PLANES // STEP + 2,)),
             pltpu.SemaphoreType.DMA((10,)),
             pltpu.SemaphoreType.DMA((10,)),
         ],
@@ -614,32 +662,25 @@
         ),
         name="prepare",
     )(*(pltpu.with_memory_space_constraint(v, pltpu.HBM) for v in (density, sx, sy)))
-    whole = lambda array: pl.BlockSpec(array.shape, lambda g: (0,) * array.ndim, pipeline_mode=pl.Buffered(1))
     tables = (colx, ycoef, scal, rh, er, lch, lcl, wcat, gxh, gxl)
     detail, local, coarse = pl.pallas_call(
         main_kernel,
-        grid=(PLANES // STEP,),
         out_shape=(f32(PLANES, FINE, FINE), f32(PLANES, LANES, LANES), f32(PLANES, LANES, LANES)),
-        in_specs=[
-            pl.BlockSpec((STEP, FINE, LANES), lambda g: (g, 0, 0)),
-            pl.BlockSpec((STEP, FINE, LANES), lambda g: (g, 0, 1)),
-        ]
-        + [whole(t) for t in tables],
-        out_specs=(
-            pl.BlockSpec((STEP, FINE, FINE), lambda g: (g, 0, 0)),
-            pl.BlockSpec((STEP, LANES, LANES), lambda g: (g, 0, 0)),
-            pl.BlockSpec((STEP, LANES, LANES), lambda g: (g, 0, 0)),
-        ),
+        in_specs=[vmem] * (1 + len(tables)),
+        out_specs=(hbm, vmem, vmem),
         scratch_shapes=[
             pltpu.VMEM((7, LANES, LANES), F32),
-            pltpu.VMEM((2, LANES + 16, LANES), F32),
-            pltpu.VMEM((2, LANES + 16, LANES), F32),
-            pltpu.VMEM((2, LANES + 16, LANES), F32),
-            pltpu.VMEM((2, FINE, LANES), F32),
+            pltpu.VMEM((PER, 2, LANES + 16, LANES), F32),
+            pltpu.VMEM((PER, 2, LANES + 16, LANES), F32),
+            pltpu.VMEM((PER, 2, LANES + 16, LANES), F32),
+            pltpu.VMEM((2, PER, 2, FINE, LANES), F32),
+            pltpu.VMEM((2, PER, LANES, FINE + LANES), BF16),
+            pltpu.VMEM((2, PER, LANES, FINE + LANES), BF16),
+            pltpu.SemaphoreType.DMA((2, 2)),
         ],
         compiler_params=pltpu.CompilerParams(vmem_limit_bytes=32 * MIB),
         name="main",
-    )(box, box, *tables)
+    )(box, *tables)
     mid, outer_l, outer_r = pl.pallas_call(
         functools.partial(exchange_kernel, nx, ny),
         out_shape=(f32(PLANES, LANES, LANES), bf16(LANES, FINE), bf16(PLANES, FINE, LANES)),
@@ -650,11 +691,15 @@
             pltpu.VMEM((nx - 1, PLANES, LANES), F32),
             pltpu.VMEM((2, PLANES, LANES), F32),
             pltpu.VMEM((ny - 1, PLANES, LANES), F32),
+            pltpu.VMEM((2, 8, LANES), F32),
+            pltpu.VMEM((ny - 1, 8, LANES), F32),
             pltpu.VMEM((2, PLANES, LANES), F32),
             pltpu.VMEM((LANES, LANES), F32),
             pltpu.VMEM((LANES, LANES), F32),
             pltpu.SemaphoreType.DMA((nx - 1,)),
             pltpu.SemaphoreType.DMA((nx - 1,)),
+            pltpu.SemaphoreType.DMA((ny - 1,)),
+            pltpu.SemaphoreType.DMA((ny - 1,)),
             pltpu.SemaphoreType.DMA((ny - 1,)),
             pltpu.SemaphoreType.DMA((ny - 1,)),
         ],

time: 45.1 us -> 42.4 us (0.940)
  Pallas kernels: 44.1 us -> 41.7 us
    pallas_call x1, Pallas kernels: 12.1 us -> 9.84 us  [per_device(): pl.pallas_call(main_kernel, out_shape=(f32(PLANES, FINE, FINE), f32(PLANE...]
where the time goes in v2:
time: 42.4 us; the launch traced here: 42.3 us
  Pallas kernels  41.7 us (98%)
  between operations  0.65 us (2%)
    pallas_call x1, Pallas kernels, per_device(): pl.pallas_call(functools.partial(prepare_kernel, nx, ny), out_shape=(f32(...  16.8 us
    pallas_call x1, Pallas kernels, per_device(): pl.pallas_call(functools.partial(exchange_kernel, nx, ny), out_shape=(f32...  12.7 us
    pallas_call x1, Pallas kernels, per_device(): pl.pallas_call(main_kernel, out_shape=(f32(PLANES, FINE, FINE), f32(PLANE...  9.84 us
    pallas_call x1, Pallas kernels, per_device(): pl.pallas_call(final_kernel, grid=(PLANES // 8,), out_shape=f32(PLANES, L...  2.34 us

profile of v2, /device:TPU:1, one launch (start us, length us, event | category | flops | bytes accessed | tf_op | source)
XLA Modules:
  0.0 42.3 jit_solution(5170449137062364699)
XLA Ops:
  0.6 16.8 %prepare.1 = (f32[128,128]{1,0:T(8,128)S(1)}, f32[8,256]{1,0:T(8,128)S(1)}, f32[8,128]{1,0:T(8,128)S(1)}, f32[24,128]{1,0:T(8,128)S(1)}, f32[24,128]{1,0:T(8,128...) custom-call(f32[32,256,256]{2,1,0:T(8,128)} %dens.1, ...), custom_call_target="tpu_custom_call" | custom-call | tf_op jit(solution)/shard_map/prepare/pallas_call | solution.py:632
  17.5 9.8 %main.1 = (f32[32,256,256]{2,1,0:T(8,128)}, f32[32,128,128]{2,1,0:T(8,128)S(1)}, f32[32,128,128]{2,1,0:T(8,128)S(1)}) custom-call(f32[2,32,256,128]{3,2,1,0:T(8,128)S(1)} %get-tuple-element.22.box, f32[128,128]{1,0:T(8,128)S(1)} %get-tuple-element.23.colx, f32[8,256]{1,0:T(8,128)S(1)} %get-tuple-element.24.ycoef, f32[8,128]{1,0:T(8,128)S(1)} %get-tuple-element.25.scal, ...), custom_call_target="tpu_custom_call" | custom-call | tf_op jit(solution)/shard_map/main/pallas_call | solution.py:666
  27.3 12.7 %exchange.1 = (f32[32,128,128]{2,1,0:T(8,128)S(1)}, bf16[128,256]{1,0:T(8,128)(2,1)S(1)}, bf16[32,256,128]{2,1,0:T(8,128)(2,1)S(1)}) custom-call(f32[32,128,128]{2,1,0:T(8,128)S(1)} %get-tuple-element.34.local, f32[32,128,128]{2,1,0:T(8,128)S(1)} %get-tuple-element.35.coarse, f32[128,128]{1,0:T(8,128)S(1)} %get-tuple-element.23.colx, ...), custom_call_target="tpu_custom_call" | custom-call | tf_op jit(solution)/shard_map/exchange/pallas_call | solution.py:684
  40.0 2.3 %final.1 = f32[32,128,128]{2,1,0:T(8,128)} custom-call(f32[32,128,128]{2,1,0:T(8,128)S(1)} %get-tuple-element.39.mid, bf16[128,256]{1,0:T(8,128)(2,1)S(1)} %get-tuple-element.40.outer_l, bf16[32,256,128]{2,1,0:T(8,128)(2,1)S(1)} %get-tuple-element.41.outer_r), custom_call_target="tpu_custom_call" | custom-call | tf_op jit(solution)/shard_map/final/pallas_call | solution.py:711

commit v3 on v2

--- a/solution.py
+++ b/solution.py
@@ -504,7 +504,8 @@
 
 def exchange_kernel(
     nx, ny, local, coarse, colx, scal, cf, cb, packed, mid, outer_l, outer_r,
-    xs, xr, ys, yr, cs, cr, sums, uwide, pwide, sx_sem, rx_sem, sy_sem, ry_sem, sc_sem, rc_sem,
+    xs, xr, ys, yr, cs, cr, ks, kr, sums, uwide, pwide,
+    sx_sem, rx_sem, sy_sem, ry_sem, sc_sem, rc_sem, sk_sem, rk_sem,
 ):
     p, r = lax.axis_index("gx"), lax.axis_index("gy")
     barrier = pltpu.get_barrier_semaphore()
@@ -512,8 +513,22 @@
         pl.semaphore_signal(barrier, inc=1, device_id=(lax.rem(p + k, nx), r), device_id_type=MESH)
     for k in range(1, ny):
         pl.semaphore_signal(barrier, inc=1, device_id=(p, lax.rem(r + k, ny)), device_id_type=MESH)
-    xs[0] = local[:, LANES - 1, :] * scal[S_FX : S_FX + 1, :]
-    xs[1] = local[:, 0, :] * scal[S_BX : S_BX + 1, :]
+    tail, front = local[:, LANES - 1, :], local[:, 0, :]
+    xs[0] = tail * scal[S_FX : S_FX + 1, :]
+    xs[1] = front * scal[S_BX : S_BX + 1, :]
+    ends = jnp.concatenate([tail, front, tail, front], axis=0).T
+    lane_1 = iota((1, LANES), 1)
+
+    def spread_planes(row):
+        row = jnp.where(lane_1 < PLANES, row, 0.0)
+        row = row + pltpu.roll(row, PLANES, 1)
+        return row + pltpu.roll(row, 2 * PLANES, 1)
+
+    ks[...] = jnp.zeros((2, 8, LANES), F32)
+    for n, at in enumerate((LANES - 1, 0)):
+        corner = ends[at : at + 1, :]
+        ks[0, n : n + 1, :] = spread_planes(corner) * scal[S_FX : S_FX + 1, :]
+        ks[1, n : n + 1, :] = spread_planes(pltpu.roll(corner, LANES - PLANES, 1)) * scal[S_BX : S_BX + 1, :]
     uwide[...] = column(colx[...], X_U)
     pwide[...] = column(colx[...], X_PSI)
 
@@ -541,6 +556,7 @@
             backward = backward + cb[row, :] * values
         return forward, backward
 
+
     lane = iota((PLANES, LANES), 1)
     blocks = LANES // PLANES
 
@@ -559,21 +575,20 @@
     ys[0] = last * scale_f
     ys[1] = head * scale_b
     pl.semaphore_wait(barrier, nx + ny - 2)
+    k_copies = start(ks, kr, sk_sem, rk_sem, p, nx, lambda i: (i, r))
     x_copies = start(xs, xr, sx_sem, rx_sem, p, nx, lambda i: (i, r))
     y_copies = start(ys, yr, sy_sem, ry_sem, r, ny, lambda j: (p, j))
 
+    corner_f, corner_b = gather(k_copies, kr, p, nx, 0)
+    cs[...] = jnp.zeros((2, 8, LANES), F32)
+    cs[0, 0:1, :] = corner_f[0:1, :] * scale_f
+    cs[0, 1:2, :] = corner_b[0:1, :] * scale_f
+    cs[1, 0:1, :] = corner_f[1:2, :] * scale_b
+    cs[1, 1:2, :] = corner_b[1:2, :] * scale_b
+    c_copies = start(cs, cr, sc_sem, rc_sem, r, ny, lambda j: (p, j))
     forward, backward = gather(x_copies, xr, p, nx, 0)
     sums[0] = forward
     sums[1] = backward
-    across_f = jnp.concatenate([forward] * blocks, axis=0).T
-    across_b = jnp.concatenate([backward] * blocks, axis=0).T
-    end = slice(LANES - 1, LANES)
-    cs[...] = jnp.zeros((2, 8, LANES), F32)
-    cs[0, 0:1, :] = across_f[end, :] * scale_f
-    cs[0, 1:2, :] = across_b[end, :] * scale_f
-    cs[1, 0:1, :] = across_f[0:1, :] * scale_b
-    cs[1, 1:2, :] = across_b[0:1, :] * scale_b
-    c_copies = start(cs, cr, sc_sem, rc_sem, r, ny, lambda j: (p, j))
 
     edge = jnp.where(
         (iota((LANES, LANES), 0) // PLANES) % 2 == 0,
@@ -609,16 +624,23 @@
     both = jnp.where(lane < 2 * PLANES, high, pltpu.roll(both - high, 2 * PLANES, 1))
     outer_l[:, 0:LANES] = both.astype(BF16)
     outer_l[:, LANES:] = both.astype(BF16)
-    for copy in x_copies + y_copies + c_copies:
+    for copy in k_copies + x_copies + y_copies + c_copies:
         copy.wait_send()
 
 
-def final_kernel(mid, outer_l, outer_r, out):
-    for z in range(0, mid.shape[0], 2):
-        pair = jnp.concatenate([outer_r[z], outer_r[z + 1]], axis=1)
-        update = mxu(outer_l[...], pair)
-        out[z] = mid[z] + update[:, :LANES]
-        out[z + 1] = mid[z + 1] + update[:, LANES:]
+def final_kernel(mid, outer_l, outer_r, out, total, sem):
+    writes = []
+    for g in range(PLANES // 8):
+        planes = pl.ds(g * 8, 8)
+        for k in range(g * 8, g * 8 + 8, 2):
+            pair = jnp.concatenate([outer_r[k], outer_r[k + 1]], axis=1)
+            update = mxu(outer_l[...], pair)
+            total[k] = mid[k] + update[:, :LANES]
+            total[k + 1] = mid[k + 1] + update[:, LANES:]
+        writes.append(pltpu.make_async_copy(total.at[planes], out.at[planes], sem.at[g]))
+        writes[-1].start()
+    for write in writes:
+        write.wait()
 
 
 def per_device(nx, ny, density, spacing_x, spacing_y):
@@ -693,6 +715,8 @@
             pltpu.VMEM((ny - 1, PLANES, LANES), F32),
             pltpu.VMEM((2, 8, LANES), F32),
             pltpu.VMEM((ny - 1, 8, LANES), F32),
+            pltpu.VMEM((2, 8, LANES), F32),
+            pltpu.VMEM((nx - 1, 8, LANES), F32),
             pltpu.VMEM((2, PLANES, LANES), F32),
             pltpu.VMEM((LANES, LANES), F32),
             pltpu.VMEM((LANES, LANES), F32),
@@ -702,6 +726,8 @@
             pltpu.SemaphoreType.DMA((ny - 1,)),
             pltpu.SemaphoreType.DMA((ny - 1,)),
             pltpu.SemaphoreType.DMA((ny - 1,)),
+            pltpu.SemaphoreType.DMA((nx - 1,)),
+            pltpu.SemaphoreType.DMA((nx - 1,)),
         ],
         compiler_params=pltpu.CompilerParams(
             collective_id=1, has_side_effects=True, vmem_limit_bytes=32 * MIB
@@ -710,15 +736,11 @@
     )(local, coarse, colx, scal, cf, cb, packed)
     coarse_new = pl.pallas_call(
         final_kernel,
-        grid=(PLANES // 8,),
         out_shape=f32(PLANES, LANES, LANES),
-        in_specs=[
-            pl.BlockSpec((8, LANES, LANES), lambda g: (g, 0, 0)),
-            pl.BlockSpec((LANES, FINE), lambda g: (0, 0)),
-            pl.BlockSpec((8, FINE, LANES), lambda g: (g, 0, 0)),
-        ],
-        out_specs=pl.BlockSpec((8, LANES, LANES), lambda g: (g, 0, 0)),
-        compiler_params=pltpu.CompilerParams(vmem_limit_bytes=32 * MIB),
+        in_specs=[vmem] * 3,
+        out_specs=hbm,
+        scratch_shapes=[pltpu.VMEM((PLANES, LANES, LANES), F32), pltpu.SemaphoreType.DMA((PLANES // 8,))],
+        compiler_params=pltpu.CompilerParams(vmem_limit_bytes=16 * MIB),
         name="final",
     )(mid, outer_l, outer_r)
     return detail, coarse_new

time: 42.4 us -> 41.1 us (0.969)
  Pallas kernels: 41.7 us -> 40.3 us
    pallas_call x1, Pallas kernels: 2.34 us -> 1.62 us  [per_device(): pl.pallas_call(final_kernel, out_shape=f32(PLANES, LANES, LANES), in_spec...]
    pallas_call x1, Pallas kernels: 12.7 us -> 12 us  [per_device(): pl.pallas_call(functools.partial(exchange_kernel, nx, ny), out_shape=(f32...]
where the time goes in v3:
time: 41.1 us; the launch traced here: 41 us
  Pallas kernels  40.3 us (98%)
  between operations  0.65 us (2%)
    pallas_call x1, Pallas kernels, per_device(): pl.pallas_call(functools.partial(prepare_kernel, nx, ny), out_shape=(f32(...  16.8 us
    pallas_call x1, Pallas kernels, per_device(): pl.pallas_call(functools.partial(exchange_kernel, nx, ny), out_shape=(f32...  12 us
    pallas_call x1, Pallas kernels, per_device(): pl.pallas_call(main_kernel, out_shape=(f32(PLANES, FINE, FINE), f32(PLANE...  9.84 us
    pallas_call x1, Pallas kernels, per_device(): pl.pallas_call(final_kernel, out_shape=f32(PLANES, LANES, LANES), in_spec...  1.62 us

profile of v3, /device:TPU:1, one launch (start us, length us, event | category | flops | bytes accessed | tf_op | source)
XLA Modules:
  0.0 41.0 jit_solution(5502656040980976586)
XLA Ops:
  0.6 16.8 %prepare.1 = (f32[128,128]{1,0:T(8,128)S(1)}, f32[8,256]{1,0:T(8,128)S(1)}, f32[8,128]{1,0:T(8,128)S(1)}, f32[24,128]{1,0:T(8,128)S(1)}, f32[24,128]{1,0:T(8,128...) custom-call(f32[32,256,256]{2,1,0:T(8,128)} %dens.1, ...), custom_call_target="tpu_custom_call" | custom-call | tf_op jit(solution)/shard_map/prepare/pallas_call | solution.py:654
  17.5 9.8 %main.1 = (f32[32,256,256]{2,1,0:T(8,128)}, f32[32,128,128]{2,1,0:T(8,128)S(1)}, f32[32,128,128]{2,1,0:T(8,128)S(1)}) custom-call(f32[2,32,256,128]{3,2,1,0:T(8,128)S(1)} %get-tuple-element.22.box, f32[128,128]{1,0:T(8,128)S(1)} %get-tuple-element.23.colx, f32[8,256]{1,0:T(8,128)S(1)} %get-tuple-element.24.ycoef, f32[8,128]{1,0:T(8,128)S(1)} %get-tuple-element.25.scal, ...), custom_call_target="tpu_custom_call" | custom-call | tf_op jit(solution)/shard_map/main/pallas_call | solution.py:688
  27.3 12.0 %exchange.1 = (f32[32,128,128]{2,1,0:T(8,128)S(1)}, bf16[128,256]{1,0:T(8,128)(2,1)S(1)}, bf16[32,256,128]{2,1,0:T(8,128)(2,1)S(1)}) custom-call(f32[32,128,128]{2,1,0:T(8,128)S(1)} %get-tuple-element.34.local, f32[32,128,128]{2,1,0:T(8,128)S(1)} %get-tuple-element.35.coarse, f32[128,128]{1,0:T(8,128)S(1)} %get-tuple-element.23.colx, ...), custom_call_target="tpu_custom_call" | custom-call | tf_op jit(solution)/shard_map/exchange/pallas_call | solution.py:706
  39.4 1.6 %final.1 = f32[32,128,128]{2,1,0:T(8,128)} custom-call(f32[32,128,128]{2,1,0:T(8,128)S(1)} %get-tuple-element.39.mid, bf16[128,256]{1,0:T(8,128)(2,1)S(1)} %get-tuple-element.40.outer_l, bf16[32,256,128]{2,1,0:T(8,128)(2,1)S(1)} %get-tuple-element.41.outer_r), custom_call_target="tpu_custom_call" | custom-call | tf_op jit(solution)/shard_map/final/pallas_call | solution.py:737

commit v4 on v3

--- a/solution.py
+++ b/solution.py
@@ -398,14 +398,13 @@
 
 def main_kernel(
     box, colx, ycoef, scal, rh, er, lch, lcl, wcat, gxh, gxl,
-    detail, local, coarse, wide, se_buf, de_buf, do_buf, woven, high, low, sem,
+    detail, local, wide, se_buf, de_buf, do_buf, woven, high, low, sem,
 ):
     for k in range(7):
         wide[k] = column(colx[...], k)
     lane = iota((LANES, LANES), 1)
     odd = (lane & 1) == 1
     inner = lane < LANES - 1
-    pick = (2 * lane) & (LANES - 1)
     wrm = scal[S_WRM : S_WRM + 1, :]
     body, before, after = pl.ds(8, LANES), pl.ds(7, LANES), pl.ds(9, LANES)
     turns = PLANES // PER
@@ -442,11 +441,6 @@
             hi, lo = split(load)
             high[slot, k, :, part] = hi
             low[slot, k, :, part] = lo
-        coarse[z] = jnp.where(
-            lane < LANES // 2,
-            jnp.take_along_axis(e[0], pick, axis=1, mode="promise_in_bounds"),
-            jnp.take_along_axis(e[1], pick, axis=1, mode="promise_in_bounds"),
-        )
         mine = (lane & (PLANES - 1)) == z
         high[slot, k, :, FINE:] = jnp.where(mine, lch[...].astype(F32), 0.0).astype(BF16)
         low[slot, k, :, FINE:] = jnp.where(mine, lcl[...].astype(F32), 0.0).astype(BF16)
@@ -503,7 +497,7 @@
 
 
 def exchange_kernel(
-    nx, ny, local, coarse, colx, scal, cf, cb, packed, mid, outer_l, outer_r,
+    nx, ny, local, box, colx, scal, cf, cb, packed, mid, outer_l, outer_r,
     xs, xr, ys, yr, cs, cr, ks, kr, sums, uwide, pwide,
     sx_sem, rx_sem, sy_sem, ry_sem, sc_sem, rc_sem, sk_sem, rk_sem,
 ):
@@ -598,9 +592,19 @@
     edge_l = edge - edge_h
     plane_of = iota((LANES, LANES), 0) % PLANES
 
+    lane_w = iota((LANES, LANES), 1)
+    pick = (2 * lane_w) & (LANES - 1)
+
     def x_part(z, carry):
         row = pl.ds(z, 1)
-        mid[z] = local[z] + coarse[z] + uwide[...] * sums[0, row, :] + pwide[...] * sums[1, row, :]
+        left, right = (
+            jnp.take_along_axis(
+                box[t, z, pl.ds(0, LANES, stride=2), :], pick, axis=1, mode="promise_in_bounds"
+            )
+            for t in range(2)
+        )
+        coarse = jnp.where(lane_w < LANES // 2, left, right)
+        mid[z] = local[z] + coarse + uwide[...] * sums[0, row, :] + pwide[...] * sums[1, row, :]
         outer_r[z, 0:LANES, :] = jnp.where(plane_of == z, edge_h, 0.0).astype(BF16)
         outer_r[z, LANES:, :] = jnp.where(plane_of == z, edge_l, 0.0).astype(BF16)
         return carry
@@ -685,11 +689,11 @@
         name="prepare",
     )(*(pltpu.with_memory_space_constraint(v, pltpu.HBM) for v in (density, sx, sy)))
     tables = (colx, ycoef, scal, rh, er, lch, lcl, wcat, gxh, gxl)
-    detail, local, coarse = pl.pallas_call(
+    detail, local = pl.pallas_call(
         main_kernel,
-        out_shape=(f32(PLANES, FINE, FINE), f32(PLANES, LANES, LANES), f32(PLANES, LANES, LANES)),
+        out_shape=(f32(PLANES, FINE, FINE), f32(PLANES, LANES, LANES)),
         in_specs=[vmem] * (1 + len(tables)),
-        out_specs=(hbm, vmem, vmem),
+        out_specs=(hbm, vmem),
         scratch_shapes=[
             pltpu.VMEM((7, LANES, LANES), F32),
             pltpu.VMEM((PER, 2, LANES + 16, LANES), F32),
@@ -733,7 +737,7 @@
             collective_id=1, has_side_effects=True, vmem_limit_bytes=32 * MIB
         ),
         name="exchange",
-    )(local, coarse, colx, scal, cf, cb, packed)
+    )(local, box, colx, scal, cf, cb, packed)
     coarse_new = pl.pallas_call(
         final_kernel,
         out_shape=f32(PLANES, LANES, LANES),

time: 41.1 us -> 40.8 us (level)
  no operation moved by 1% of the time
where the time goes in v4:
time: 40.8 us; the launch traced here: 40.6 us
  Pallas kernels  40 us (98%)
  between operations  0.65 us (2%)
    pallas_call x1, Pallas kernels, per_device(): pl.pallas_call(functools.partial(prepare_kernel, nx, ny), out_shape=(f32(...  16.8 us
    pallas_call x1, Pallas kernels, per_device(): pl.pallas_call(functools.partial(exchange_kernel, nx, ny), out_shape=(f32...  12 us
    pallas_call x1, Pallas kernels, per_device(): pl.pallas_call(main_kernel, out_shape=(f32(PLANES, FINE, FINE), f32(PLANE...  9.51 us
    pallas_call x1, Pallas kernels, per_device(): pl.pallas_call(final_kernel, out_shape=f32(PLANES, LANES, LANES), in_spec...  1.62 us

profile of v4, /device:TPU:1, one launch (start us, length us, event | category | flops | bytes accessed | tf_op | source)
XLA Modules:
  0.0 40.6 jit_solution(6230574414522461815)
XLA Ops:
  0.6 16.8 %prepare.1 = (f32[128,128]{1,0:T(8,128)S(1)}, f32[8,256]{1,0:T(8,128)S(1)}, f32[8,128]{1,0:T(8,128)S(1)}, f32[24,128]{1,0:T(8,128)S(1)}, f32[24,128]{1,0:T(8,128...) custom-call(f32[32,256,256]{2,1,0:T(8,128)} %dens.1, ...), custom_call_target="tpu_custom_call" | custom-call | tf_op jit(solution)/shard_map/prepare/pallas_call | solution.py:658
  17.5 9.5 %main.1 = (f32[32,256,256]{2,1,0:T(8,128)}, f32[32,128,128]{2,1,0:T(8,128)S(1)}) custom-call(f32[2,32,256,128]{3,2,1,0:T(8,128)S(1)} %get-tuple-element.21.box, f32[128,128]{1,0:T(8,128)S(1)} %get-tuple-element.22.colx, f32[8,256]{1,0:T(8,128)S(1)} %get-tuple-element.23.ycoef, f32[8,128]{1,0:T(8,128)S(1)} %get-tuple-element.24.scal, ...), custom_call_target="tpu_custom_call" | custom-call | tf_op jit(solution)/shard_map/main/pallas_call | solution.py:692
  27.0 12.0 %exchange.1 = (f32[32,128,128]{2,1,0:T(8,128)S(1)}, bf16[128,256]{1,0:T(8,128)(2,1)S(1)}, bf16[32,256,128]{2,1,0:T(8,128)(2,1)S(1)}) custom-call(f32[32,128,128]{2,1,0:T(8,128)S(1)} %get-tuple-element.33.local, f32[2,32,256,128]{3,2,1,0:T(8,128)S(1)} %get-tuple-element.21.box, f32[128,128]{1,0:T(8,128)S(1)} %get-tuple-element.22.colx, ...), custom_call_target="tpu_custom_call" | custom-call | tf_op jit(solution)/shard_map/exchange/pallas_call | solution.py:710
  39.0 1.6 %final.1 = f32[32,128,128]{2,1,0:T(8,128)} custom-call(f32[32,128,128]{2,1,0:T(8,128)S(1)} %get-tuple-element.37.mid, bf16[128,256]{1,0:T(8,128)(2,1)S(1)} %get-tuple-element.38.outer_l, bf16[32,256,128]{2,1,0:T(8,128)(2,1)S(1)} %get-tuple-element.39.outer_r), custom_call_target="tpu_custom_call" | custom-call | tf_op jit(solution)/shard_map/final/pallas_call | solution.py:741

commit v5 on v4

--- a/solution.py
+++ b/solution.py
@@ -523,21 +523,17 @@
         corner = ends[at : at + 1, :]
         ks[0, n : n + 1, :] = spread_planes(corner) * scal[S_FX : S_FX + 1, :]
         ks[1, n : n + 1, :] = spread_planes(pltpu.roll(corner, LANES - PLANES, 1)) * scal[S_BX : S_BX + 1, :]
-    uwide[...] = column(colx[...], X_U)
-    pwide[...] = column(colx[...], X_PSI)
 
     def start(sent, got, send_sem, recv_sem, own, count, target):
-        copies = []
-        for k in range(1, count):
+        copies = [None] * (count - 1)
+        for k in sorted(range(1, count), key=lambda k: abs(count - 2 * k)):
             wraps = jnp.where(own + k >= count, 1, 0)
-            copies.append(
-                pltpu.make_async_remote_copy(
-                    src_ref=sent.at[wraps], dst_ref=got.at[k - 1],
-                    send_sem=send_sem.at[k - 1], recv_sem=recv_sem.at[k - 1],
-                    device_id=target(lax.rem(own + k, count)), device_id_type=MESH,
-                )
+            copies[k - 1] = pltpu.make_async_remote_copy(
+                src_ref=sent.at[wraps], dst_ref=got.at[k - 1],
+                send_sem=send_sem.at[k - 1], recv_sem=recv_sem.at[k - 1],
+                device_id=target(lax.rem(own + k, count)), device_id_type=MESH,
             )
-            copies[-1].start()
+            copies[k - 1].start()
         return copies
 
     def gather(copies, got, own, count, low):
@@ -580,6 +576,8 @@
     cs[1, 0:1, :] = corner_f[1:2, :] * scale_b
     cs[1, 1:2, :] = corner_b[1:2, :] * scale_b
     c_copies = start(cs, cr, sc_sem, rc_sem, r, ny, lambda j: (p, j))
+    uwide[...] = column(colx[...], X_U)
+    pwide[...] = column(colx[...], X_PSI)
     forward, backward = gather(x_copies, xr, p, nx, 0)
     sums[0] = forward
     sums[1] = backward
@@ -610,6 +608,8 @@
         return carry
 
     lax.fori_loop(0, PLANES, x_part, 0, unroll=2)
+    for copy in k_copies + x_copies + y_copies + c_copies:
+        copy.wait_send()
     u_x, psi_x = packed[0], packed[1]
     forward, backward = gather(y_copies, yr, r, ny, nx)
     extra_f, extra_b = gather(c_copies, cr, r, ny, nx)
@@ -628,8 +628,6 @@
     both = jnp.where(lane < 2 * PLANES, high, pltpu.roll(both - high, 2 * PLANES, 1))
     outer_l[:, 0:LANES] = both.astype(BF16)
     outer_l[:, LANES:] = both.astype(BF16)
-    for copy in k_copies + x_copies + y_copies + c_copies:
-        copy.wait_send()
 
 
 def final_kernel(mid, outer_l, outer_r, out, total, sem):

time: 40.8 us -> 40.6 us (level)
  no operation moved by 1% of the time
where the time goes in v5:
time: 40.6 us; the launch traced here: 40.5 us
  Pallas kernels  39.8 us (98%)
  between operations  0.65 us (2%)
    pallas_call x1, Pallas kernels, per_device(): pl.pallas_call(functools.partial(prepare_kernel, nx, ny), out_shape=(f32(...  16.8 us
    pallas_call x1, Pallas kernels, per_device(): pl.pallas_call(functools.partial(exchange_kernel, nx, ny), out_shape=(f32...  11.8 us
    pallas_call x1, Pallas kernels, per_device(): pl.pallas_call(main_kernel, out_shape=(f32(PLANES, FINE, FINE), f32(PLANE...  9.51 us
    pallas_call x1, Pallas kernels, per_device(): pl.pallas_call(final_kernel, out_shape=f32(PLANES, LANES, LANES), in_spec...  1.62 us

profile of v5, /device:TPU:1, one launch (start us, length us, event | category | flops | bytes accessed | tf_op | source)
XLA Modules:
  0.0 40.5 jit_solution(11375841180060538361)
XLA Ops:
  0.6 16.8 %prepare.1 = (f32[128,128]{1,0:T(8,128)S(1)}, f32[8,256]{1,0:T(8,128)S(1)}, f32[8,128]{1,0:T(8,128)S(1)}, f32[24,128]{1,0:T(8,128)S(1)}, f32[24,128]{1,0:T(8,128...) custom-call(f32[32,256,256]{2,1,0:T(8,128)} %dens.1, ...), custom_call_target="tpu_custom_call" | custom-call | tf_op jit(solution)/shard_map/prepare/pallas_call | solution.py:656
  17.5 9.5 %main.1 = (f32[32,256,256]{2,1,0:T(8,128)}, f32[32,128,128]{2,1,0:T(8,128)S(1)}) custom-call(f32[2,32,256,128]{3,2,1,0:T(8,128)S(1)} %get-tuple-element.21.box, f32[128,128]{1,0:T(8,128)S(1)} %get-tuple-element.22.colx, f32[8,256]{1,0:T(8,128)S(1)} %get-tuple-element.23.ycoef, f32[8,128]{1,0:T(8,128)S(1)} %get-tuple-element.24.scal, ...), custom_call_target="tpu_custom_call" | custom-call | tf_op jit(solution)/shard_map/main/pallas_call | solution.py:690
  27.0 11.8 %exchange.1 = (f32[32,128,128]{2,1,0:T(8,128)S(1)}, bf16[128,256]{1,0:T(8,128)(2,1)S(1)}, bf16[32,256,128]{2,1,0:T(8,128)(2,1)S(1)}) custom-call(f32[32,128,128]{2,1,0:T(8,128)S(1)} %get-tuple-element.33.local, f32[2,32,256,128]{3,2,1,0:T(8,128)S(1)} %get-tuple-element.21.box, f32[128,128]{1,0:T(8,128)S(1)} %get-tuple-element.22.colx, ...), custom_call_target="tpu_custom_call" | custom-call | tf_op jit(solution)/shard_map/exchange/pallas_call | solution.py:708
  38.8 1.6 %final.1 = f32[32,128,128]{2,1,0:T(8,128)} custom-call(f32[32,128,128]{2,1,0:T(8,128)S(1)} %get-tuple-element.37.mid, bf16[128,256]{1,0:T(8,128)(2,1)S(1)} %get-tuple-element.38.outer_l, bf16[32,256,128]{2,1,0:T(8,128)(2,1)S(1)} %get-tuple-element.39.outer_r), custom_call_target="tpu_custom_call" | custom-call | tf_op jit(solution)/shard_map/final/pallas_call | solution.py:739
